TPU v7x, 32 devices: a whole 2x2x4 slice. The times are simulated.
32 devices in a mesh: dp: 8 (over z, x), seq: 4 (over y, core).
Axes of the slice: x: 2, y: 2, z: 4, core: 2. Of those that a mesh axis runs over, the one named last changes fastest.
Arguments:
- residual_tiles: bfloat16 [8, 1024, 1024], P('dp', 'seq'), may hold values from -16 to 16
- picture_label_tile: int32 [8, 1024], P('dp', 'seq'), may hold values from 0 to 11, never falling along the last dimension, each value on 1 to 512 neighbouring positions
- prenorm_multiplier: float32 [1024], replicated, may hold values from 0.5 to 1.5
- triple_projector: bfloat16 [1024, 3072], P('dp'), may hold values from -0.25 to 0.25
- logit_scaling: float32 [16], replicated, may hold values from 0.3 to 30
- final_projector: bfloat16 [1024, 1024], P('dp'), may hold values from -0.1875 to 0.1875
- binarizer_projector: bfloat16 [1024, 18], replicated, may hold values from -0.1875 to 0.1875
- binarizer_offset: float32 [18], replicated, may hold values from -1 to 1
Outputs:
- mixed: bfloat16 [8, 1024, 1024], P('dp', 'seq')
- bit_codes: float32 [8, 18, 1024], P('dp', None, 'seq')
- code_entropy: float32 [18], replicated
Inputs may be any that keep to these rules, and one draw needn't show every extreme that they name: `picture_label_tile`: in each pack image numbers never fall, every image number of 0 to 11 occurs, and an image has at most 512 patches.
All inputs are finite; a program needn't handle non-finite values.
Results may differ from a plain program's by a relative error of at most 0.0053.
The roundings to bfloat16 on the way count: a program that leaves them out, or rounds other values in their place, can miss the bound.
Values may be sent and summed in bfloat16 or wider, within the bound.
A program may use at most 64 MiB of HBM per device.

v0:
```python
import functools
import math

import jax
import jax.numpy as jnp
from jax import lax
from jax.experimental import pallas as pl
from jax.experimental.pallas import tpu as pltpu
from jax.sharding import PartitionSpec as P

EPS = 1e-06
MESH = pl.DeviceIdType.MESH
NEG = -1e30


def layer_kernel(
    cfg,
    x_ref,
    ids_ref,
    gain_ref,
    w_ref,
    scale_ref,
    wo_ref,
    bits_ref,
    off_ref,
    mixed_ref,
    codes_ref,
    ent_ref,
    wg,
    wog,
    xg,
    idg,
    idcol,
    normed,
    acc,
    qs,
    ks,
    vs,
    ao,
    ag,
    part1,
    part2,
    local_sem,
    wz_s,
    wz_r,
    wx_s,
    wx_r,
    oz_s,
    oz_r,
    ox_s,
    ox_r,
    oc_s,
    oc_r,
    xy_s,
    xy_r,
    xc_s,
    xc_r,
    id_s,
    id_r,
    at_s,
    at_r,
    p1_s,
    p1_r,
    p2_s,
    p2_r,
):
    nz, nx, ny, nc = cfg["nz"], cfg["nx"], cfg["ny"], cfg["nc"]
    n = ny * nc
    ndp = nz * nx
    heads, channel = cfg["heads"], cfg["channel"]
    rows, width = x_ref.shape
    shard = w_ref.shape[0]
    chunk = nx * shard
    cols = width // n
    seq_len = rows * n
    bits = bits_ref.shape[0]
    dp = lax.axis_index("dp")
    me = lax.axis_index("seq")
    z = dp // nx
    x = dp % nx
    y = me // nc
    core = me % nc

    def dp_at(zz, xx):
        return zz * nx + xx

    def seq_at(yy, cc):
        return yy * nc + cc

    def remote(src, dst, ss, rs, d, s):
        return pltpu.make_async_remote_copy(
            src_ref=src, dst_ref=dst, send_sem=ss, recv_sem=rs, device_id=(d, s), device_id_type=MESH
        )

    sends = []

    def go(c):
        c.start()
        sends.append(c)

    def arrive(slot, sem):
        remote(slot, slot, sem, sem, dp, me).wait_recv()

    parts = cfg["parts"]
    piece_rows = shard // parts

    def w_slot_of(h):
        def slot(zz, xx):
            return wg.at[zz, pl.ds(pl.multiple_of(xx * shard + h * piece_rows, piece_rows), piece_rows), :]

        return slot

    w_slots = [w_slot_of(h) for h in range(parts)]
    half_rows = rows // 2

    def x_half(member, h):
        return xg.at[member, pl.ds(h * half_rows, half_rows), :]

    def o_slot(zz, xx):
        return wog.at[core, pl.ds(pl.multiple_of(dp_at(zz, xx) * shard, shard), shard), :]

    lo = jnp.minimum(z, nz - 1 - z)

    def piece(i):
        near = z - (i + 1) // 2 if i % 2 else z + (i + 1) // 2
        far = jnp.where(z > nz - 1 - z, z - (i - lo), z + (i - lo))
        return jnp.where(i <= 2 * lo, near, far) if i else z

    def first_hops(slot, ss, rs):
        left = remote(slot(z, x), slot(z, x), ss.at[nz], rs.at[z], dp_at(jnp.maximum(z - 1, 0), x), me)
        right = remote(
            slot(z, x), slot(z, x), ss.at[nz + 1], rs.at[z], dp_at(jnp.minimum(z + 1, nz - 1), x), me
        )
        return left, right

    def next_hops(slot, ss, rs, i):
        p = piece(i)
        left = remote(slot(p, x), slot(p, x), ss.at[p], rs.at[p], dp_at(jnp.maximum(z - 1, 0), x), me)
        right = remote(
            slot(p, x), slot(p, x), ss.at[p], rs.at[p], dp_at(jnp.minimum(z + 1, nz - 1), x), me
        )
        return left, right

    line_sends = []

    def line_start(slot, ss, rs, i):
        if nz == 1:
            return
        p = piece(i)
        left, right = next_hops(slot, ss, rs, i) if i else first_hops(slot, ss, rs)
        to_left = jnp.logical_and(p >= z, z > 0)
        to_right = jnp.logical_and(p <= z, z < nz - 1)
        line_sends.append((to_left, left))
        line_sends.append((to_right, right))

        @pl.when(to_left)
        def _():
            left.start()

        @pl.when(to_right)
        def _():
            right.start()

    def across(slot, ss, rs, i):
        p = piece(i)
        for k in range(1, nx):
            go(remote(slot(p, x), slot(p, x), ss.at[p, k], rs.at[p, k], dp_at(z, (x + k) % nx), me))

    def shared(p, xx, k):
        idx = dp_at(p, xx)
        slot = o_slot(p, xx)
        return remote(slot, slot, oc_s.at[idx, k], oc_r.at[idx, k], dp, seq_at(y, (core + k) % nc))

    def share(p, xx):
        for k in range(1, nc):
            shared(p, xx, k).start()

    def w_relay(i):
        p = piece(i)
        for h, slot in enumerate(w_slots):
            arrive(slot(p, x), wz_r.at[h, p])
            line_start(slot, wz_s.at[h], wz_r.at[h], i)
            across(slot, wx_s.at[h], wx_r.at[h], i)

    def o_relay(i):
        p = piece(i)
        arrive(o_slot(p, x), oz_r.at[p])
        line_start(o_slot, oz_s, oz_r, i)
        across(o_slot, ox_s, ox_r, i)
        share(p, x)

    def o_crossed(i):
        p = piece(i)
        for k in range(1, nx):
            xx = (x - k + nx) % nx
            arrive(o_slot(p, xx), ox_r.at[p, k])
            share(p, xx)

    own = []
    for part in range(3):
        own.append(
            pltpu.make_async_copy(
                w_ref.at[:, pl.ds(pl.multiple_of(part * width + me * cols, 128), cols)],
                wg.at[
                    z,
                    pl.ds(pl.multiple_of(x * shard, shard), shard),
                    pl.ds(part * cols, cols),
                ],
                local_sem.at[part],
            )
        )
    own.append(pltpu.make_async_copy(x_ref, xg.at[me], local_sem.at[3]))
    own.append(pltpu.make_async_copy(ids_ref, idg.at[me], local_sem.at[4]))
    own.append(
        pltpu.make_async_copy(
            wo_ref.at[:, pl.ds(pl.multiple_of(core * (width // nc), 128), width // nc)],
            o_slot(z, x),
            local_sem.at[5],
        )
    )
    for c in own:
        c.start()

    barrier = pltpu.get_barrier_semaphore()

    def greet_seq(i, _):
        pl.semaphore_signal(
            barrier, inc=1, device_id=(dp, (me + i) % n), device_id_type=MESH
        )
        return 0

    def greet_dp(i, _):
        pl.semaphore_signal(
            barrier, inc=1, device_id=((dp + i) % ndp, me), device_id_type=MESH
        )
        return 0

    lax.fori_loop(1, n, greet_seq, 0)
    lax.fori_loop(1, ndp, greet_dp, 0)
    pl.semaphore_wait(barrier, n - 1 + ndp - 1)

    own[0].wait()
    own[1].wait()
    own[2].wait()
    for h, slot in enumerate(w_slots):
        line_start(slot, wz_s.at[h], wz_r.at[h], 0)
        across(slot, wx_s.at[h], wx_r.at[h], 0)
    own[4].wait()
    for i in range(1, n):
        go(remote(idg.at[me], idg.at[me], id_s.at[i], id_r.at[i], dp, (me + i) % n))
    own[3].wait()
    for h in range(2):
        for i in range(1, ny):
            own_half = x_half(me, h)
            go(remote(own_half, own_half, xy_s.at[h, i], xy_r.at[h, i], dp, seq_at((y + i) % ny, core)))
    for k in range(1, nc):
        go(remote(xg.at[me], xg.at[me], xc_s.at[0, 0, k], xc_r.at[0, 0, k], dp, seq_at(y, (core + k) % nc)))
    own[5].wait()
    line_start(o_slot, oz_s, oz_r, 0)
    across(o_slot, ox_s, ox_r, 0)
    share(z, x)

    gain = gain_ref[...]

    def norm_rows(member, h):
        base = pl.multiple_of(member * rows, rows)

        def body(b, _):
            r0 = pl.multiple_of(h * half_rows + b * 64, 64)
            wide = xg[member, pl.ds(r0, 64), :].astype(jnp.float32)
            ms = jnp.mean(wide * wide, axis=-1, keepdims=True)
            out = (wide * lax.rsqrt(ms + EPS) * gain).astype(jnp.bfloat16)
            for g in range(nz):
                normed[g, pl.ds(base + r0, 64), :] = out[:, g * chunk : (g + 1) * chunk]
            return 0

        lax.fori_loop(0, half_rows // 64, body, 0)

    def x_relay(h):
        for i in range(1, ny):
            source = seq_at((y - i + ny) % ny, core)
            slot = x_half(source, h)
            arrive(slot, xy_r.at[h, i])
            for k in range(1, nc):
                go(remote(slot, slot, xc_s.at[h, i, k], xc_r.at[h, i, k], dp, seq_at(y, (core + k) % nc)))
            norm_rows(source, h)

    def x_shared(h):
        for i in range(1, ny):
            for k in range(1, nc):
                other = seq_at((y - i + ny) % ny, (core - k + nc) % nc)
                arrive(x_half(other, h), xc_r.at[h, i, k])
                norm_rows(other, h)

    for h in range(2):
        norm_rows(me, h)
    for k in range(1, nc):
        other = seq_at(y, (core - k + nc) % nc)
        arrive(xg.at[other], xc_r.at[0, 0, k])
        for h in range(2):
            norm_rows(other, h)
    for i in range(1, nz):
        w_relay(i)
        if i == 1:
            x_relay(0)
    if nz == 1:
        x_relay(0)
    x_relay(1)
    for h in range(2):
        x_shared(h)

    for i in range(1, n):
        arrive(idg.at[(me - i + n) % n], id_r.at[i])
    for m in range(n):
        line = jnp.broadcast_to(idg[m].astype(jnp.float32), (128, rows))
        idcol[pl.ds(m * rows, rows), :] = jnp.transpose(line)
    id_row = jnp.concatenate([idg[m] for m in range(n)], axis=1).astype(jnp.float32)

    row_block = 256
    blocks = seq_len // row_block

    def project(i, first):
        zz = piece(i)
        for k in range(1, nx):
            for h, slot in enumerate(w_slots):
                arrive(slot(zz, (x - k + nx) % nx), wx_r.at[h, zz, k])

        def body(b, _):
            r = pl.ds(pl.multiple_of(b * row_block, row_block), row_block)
            prod = jnp.dot(normed[zz, r, :], wg[zz], preferred_element_type=jnp.float32)
            if first:
                acc[r, :] = prod
            else:
                acc[r, :] = acc[r, :] + prod
            return 0

        lax.fori_loop(0, blocks, body, 0)

    for i in range(nz):
        if i == max(0, nz - 2):
            for e in range(1, nz - 2):
                o_relay(e)
        project(i, i == 0)
    if nz > 2:
        o_relay(nz - 2)

    def group_of(shape, dim):
        return lax.div(lax.broadcasted_iota(jnp.int32, shape, dim), jnp.int32(channel))

    same_head = (group_of((cols, cols), 0) == group_of((cols, cols), 1)).astype(jnp.float32)
    same_head = same_head.astype(jnp.bfloat16)
    scale_row = jnp.zeros((1, cols), jnp.float32)
    for h in range(heads):
        scale_row = jnp.where(group_of((1, cols), 1) == h, scale_ref[me * heads + h], scale_row)
    scale_row = scale_row / math.sqrt(channel)

    def head_scale(values):
        square = values * values
        high = square.astype(jnp.bfloat16)
        low = (square - high.astype(jnp.float32)).astype(jnp.bfloat16)
        total = jnp.dot(high, same_head, preferred_element_type=jnp.float32) + jnp.dot(
            low, same_head, preferred_element_type=jnp.float32
        )
        return lax.rsqrt(total / channel + EPS)

    def split(b, _):
        r = pl.ds(pl.multiple_of(b * row_block, row_block), row_block)
        joined = acc[r, :].astype(jnp.bfloat16)
        q = joined[:, :cols].astype(jnp.float32)
        k = joined[:, cols : 2 * cols].astype(jnp.float32)
        qs[r, :] = (q * head_scale(q) * scale_row).astype(jnp.bfloat16)
        ks[r, :] = (k * head_scale(k)).astype(jnp.bfloat16)
        vs[r, :] = joined[:, 2 * cols :]
        return 0

    lax.fori_loop(0, blocks, split, 0)

    if nz > 1:
        o_relay(nz - 1)
    o_crossed(0)

    q_block = cfg["q_block"]
    lane_head = group_of((q_block, cols), 1)

    def stage_target(t, sign):
        dy = (t // nc + 1) % ny
        dc = (t + 1) % nc
        if sign > 0:
            return seq_at((y + dy) % ny, (core + dc) % nc)
        return seq_at((y - dy + ny) % ny, (core - dc + nc) % nc)

    def a2a(t):
        j = stage_target(t, 1)
        return remote(ao.at[j], ag.at[me], at_s.at[t], at_r.at[t], dp, j)

    def stage(t, _):
        j = stage_target(t, 1)
        for sub in range(rows // q_block):
            r = pl.ds(pl.multiple_of(j * rows + sub * q_block, q_block), q_block)
            bias = jnp.where(idcol[r, :][:, :1] == id_row, 0.0, NEG)
            qb = qs[r, :]
            out = jnp.zeros((q_block, cols), jnp.float32)
            for h in range(heads):
                mine = lane_head == h
                qh = jnp.where(mine, qb, jnp.zeros_like(qb))
                s = lax.dot_general(
                    qh, ks[...], (((1,), (1,)), ((), ())), preferred_element_type=jnp.float32
                )
                s = s + bias
                p = jnp.exp(s - jnp.max(s, axis=-1, keepdims=True))
                total = jnp.sum(p, axis=-1, keepdims=True)
                o = jnp.dot(p.astype(jnp.bfloat16), vs[...], preferred_element_type=jnp.float32)
                out = jnp.where(mine, o / total, out)
            ao[j, pl.ds(sub * q_block, q_block), :] = out.astype(jnp.bfloat16)

        @pl.when(t < n - 1)
        def _():
            a2a(t).start()

        for i in range(1, nz):

            @pl.when(t == min(i - 1, n - 1))
            def _(i=i):
                o_crossed(i)

        return 0

    lax.fori_loop(0, n, stage, 0)

    for k in range(1, nc):
        half = wog.at[(core - k + nc) % nc]
        for d in range(ndp):
            arrive(half.at[pl.ds(d * shard, shard), :], oc_r.at[d, k])
    for t in range(n - 1):
        arrive(ag.at[stage_target(t, -1)], at_r.at[t])
    ag[me] = ao[me]

    attention = jnp.concatenate([ag[m] for m in range(n)], axis=1)
    for g in range(nc):
        lanes = slice(g * (width // nc), (g + 1) * (width // nc))
        prod = jnp.dot(attention, wog[g], preferred_element_type=jnp.float32)
        mixed_ref[:, lanes] = (xg[me, :, lanes].astype(jnp.float32) + prod).astype(jnp.bfloat16)

    logits = lax.dot_general(
        bits_ref[...], mixed_ref[...], (((1,), (1,)), ((), ())), preferred_element_type=jnp.float32
    )
    eye = lax.broadcasted_iota(jnp.int32, (bits, bits), 0) == lax.broadcasted_iota(
        jnp.int32, (bits, bits), 1
    )
    offset = jnp.sum(jnp.where(eye, off_ref[...], 0.0), axis=1, keepdims=True)
    probs = jax.nn.sigmoid(4.0 * (logits + offset))
    lanes_eye = lax.broadcasted_iota(jnp.int32, (bits, 128), 0) == lax.broadcasted_iota(
        jnp.int32, (bits, 128), 1
    )
    own_sums = jnp.sum(probs, axis=1, keepdims=True)
    part1[me, :, :] = jnp.sum(jnp.where(lanes_eye, own_sums, 0.0), axis=0, keepdims=True)
    for i in range(1, n):
        go(remote(part1.at[me], part1.at[me], p1_s.at[i], p1_r.at[i], dp, (me + i) % n))
    for i in range(1, n):
        arrive(part1.at[(me - i + n) % n], p1_r.at[i])
    pack = part1[0]
    for m in range(1, n):
        pack = pack + part1[m]
    part2[dp, :, :] = pack
    for i in range(1, ndp):
        go(remote(part2.at[dp], part2.at[dp], p2_s.at[i], p2_r.at[i], (dp + i) % ndp, me))
    for i in range(1, ndp):
        arrive(part2.at[(dp - i + ndp) % ndp], p2_r.at[i])
    total = part2[0]
    for m in range(1, ndp):
        total = total + part2[m]
    marginal = total / (seq_len * ndp)
    line = marginal[:, :bits]
    ent_ref[...] = -(line * jnp.log(line) + (1.0 - line) * jnp.log(1.0 - line))
    codes = probs - jnp.sum(jnp.where(lanes_eye, marginal, 0.0), axis=1, keepdims=True)
    for b in range(bits):
        codes_ref[b] = codes[b : b + 1, :]

    for c in sends:
        c.wait_send()
    for t in range(n - 1):
        a2a(t).wait_send()
    for d in range(ndp):
        for k in range(1, nc):
            shared(d // nx, d % nx, k).wait_send()
    for cond, c in line_sends:

        @pl.when(cond)
        def _(c=c):
            c.wait_send()


def on_device(
    cfg,
    residual_tiles,
    picture_label_tile,
    prenorm_multiplier,
    triple_projector,
    logit_scaling,
    final_projector,
    binarizer_projector,
    binarizer_offset,
):
    nz, nx, ny, nc = cfg["nz"], cfg["nx"], cfg["ny"], cfg["nc"]
    n, ndp = ny * nc, nz * nx
    _, rows, width = residual_tiles.shape
    heads_all = logit_scaling.shape[0]
    bits = binarizer_projector.shape[1]
    cols = width // n
    shard = triple_projector.shape[0]
    seq_len = rows * n
    parts = 2 if shard % 32 == 0 else 1
    cfg = dict(cfg, heads=heads_all // n, channel=width // heads_all, q_block=min(256, rows), parts=parts)
    dma = pltpu.SemaphoreType.DMA
    vmem, hbm = pl.BlockSpec(memory_space=pltpu.VMEM), pl.BlockSpec(memory_space=pl.ANY)
    smem = pl.BlockSpec(memory_space=pltpu.SMEM)
    bf16, f32 = jnp.bfloat16, jnp.float32
    mixed, codes, ent = pl.pallas_call(
        functools.partial(layer_kernel, cfg),
        out_shape=(
            jax.ShapeDtypeStruct((rows, width), bf16),
            jax.ShapeDtypeStruct((bits, 1, rows), f32),
            jax.ShapeDtypeStruct((1, bits), f32),
        ),
        in_specs=[hbm, vmem, vmem, hbm, smem, hbm, vmem, vmem],
        out_specs=(vmem, vmem, vmem),
        scratch_shapes=[
            pltpu.VMEM((nz, nx * shard, 3 * cols), bf16),
            pltpu.VMEM((nc, width, width // nc), bf16),
            pltpu.VMEM((n, rows, width), bf16),
            pltpu.VMEM((n, 1, rows), jnp.int32),
            pltpu.VMEM((seq_len, 128), f32),
            pltpu.VMEM((nz, seq_len, nx * shard), bf16),
            pltpu.VMEM((seq_len, 3 * cols), f32),
            pltpu.VMEM((seq_len, cols), bf16),
            pltpu.VMEM((seq_len, cols), bf16),
            pltpu.VMEM((seq_len, cols), bf16),
            pltpu.VMEM((n, rows, cols), bf16),
            pltpu.VMEM((n, rows, cols), bf16),
            pltpu.VMEM((n, 1, 128), f32),
            pltpu.VMEM((ndp, 1, 128), f32),
            dma((6,)),
            dma((parts, nz + 2)),
            dma((parts, nz)),
            dma((parts, nz, nx)),
            dma((parts, nz, nx)),
            dma((nz + 2,)),
            dma((nz,)),
            dma((nz, nx)),
            dma((nz, nx)),
            dma((ndp, nc)),
            dma((ndp, nc)),
            dma((2, ny)),
            dma((2, ny)),
            dma((2, ny, nc)),
            dma((2, ny, nc)),
            dma((n,)),
            dma((n,)),
            dma((n,)),
            dma((n,)),
            dma((n,)),
            dma((n,)),
            dma((ndp,)),
            dma((ndp,)),
        ],
        compiler_params=pltpu.CompilerParams(
            collective_id=0, has_side_effects=True, vmem_limit_bytes=60 * 1024 * 1024
        ),
        name="layer",
    )(
        residual_tiles[0],
        picture_label_tile,
        prenorm_multiplier[None],
        triple_projector,
        logit_scaling,
        final_projector,
        binarizer_projector.T,
        binarizer_offset[None],
    )
    return mixed[None], jnp.swapaxes(codes, 0, 1), ent[0]


def solution(mesh):
    ndp, n = mesh.shape["dp"], mesh.shape["seq"]
    nx = math.isqrt(ndp // 2)
    if nx < 1 or ndp % nx:
        nx = 1
    nc = 2 if n % 2 == 0 else 1
    cfg = {"nz": ndp // nx, "nx": nx, "ny": n // nc, "nc": nc}
    return jax.shard_map(
        functools.partial(on_device, cfg),
        mesh=mesh,
        in_specs=(
            P("dp", "seq", None),
            P("dp", "seq"),
            P(),
            P("dp", None),
            P(),
            P("dp", None),
            P(),
            P(),
        ),
        out_specs=(P("dp", "seq", None), P("dp", None, "seq"), P()),
        check_vma=False,
    )
```

profile of v0, /device:TPU:0, one launch (start us, length us, event | category | flops | bytes accessed | tf_op | source)
XLA Modules:
  0.0 58.8 jit_solution(12216865507001599492)
XLA Ops:
  0.6 55.1 %layer.1 = (bf16[256,1024]{1,0:T(8,128)(2,1)}, f32[18,1,256]{2,1,0:T(1,128)}, f32[1,18]{1,0:T(1,128)}) custom-call(bf16[256,1024]{1,0:T(8,128)(2,1)} %bitcast.7, s32[1,256]{1,0:T(1,128)} %ids_ref.1, f32[1,1024]{1,0:T(1,128)} %bitcast.11, bf16[128,3072]{1,0:T(8,128)(2,1)} %w_ref.1, f32[16]{0:T(128)} %scale_ref.1, bf16[128,1024]{1,0:T(8,128)(2,1)} %wo_ref.1, ...), custom_call_target="tpu_custom_call" | custom-call | tf_op jit(solution)/shard_map/layer/pallas_call | solution.py:518
  55.7 0.0 copy-start
  55.7 1.9 %copy.14 = bf16[1,256,1024]{2,1,0:T(8,128)(2,1)} copy(bf16[1,256,1024]{2,1,0:T(8,128)(2,1)} %bitcast.8) | data formatting | bytes 1048576
  57.6 0.0 copy-done
  57.6 0.0 copy-start.1
  57.6 0.6 %copy.15 = f32[1,18,256]{2,0,1:T(1,128)} copy(f32[1,18,256]{2,0,1:T(1,128)S(1)} %bitcast.10) | data formatting | bytes 36864
  58.2 0.1 copy-done.1
  58.3 0.5 copy.16
Async XLA Ops:
  55.7 1.9 %copy-start = (f32[18,1,256]{2,1,0:T(1,128)S(1)}, f32[18,1,256]{2,1,0:T(1,128)}, u32[]{:S(2)}) copy-start(f32[18,1,256]{2,1,0:T(1,128)} %get-tuple-element.7) | copy-start | bytes 55300
  57.6 0.7 %copy-start.1 = (f32[1,18]{1,0:T(1,128)S(1)}, f32[1,18]{1,0:T(1,128)}, u32[]{:S(2)}) copy-start(f32[1,18]{1,0:T(1,128)} %get-tuple-element.8) | copy-start | bytes 220
where the time goes:
time: 59 us; the launch traced here: 58.8 us
  Pallas kernels  55.1 us (93%)
  local copies, waits for them, and re-layouts  3.05 us (5%)
  between operations  0.65 us (1%)
    pallas_call x1, Pallas kernels, on_device(): pl.pallas_call(functools.partial(layer_kernel, cfg), out_shape=(jax.Shape...  55.1 us
    unnamed x7, local copies, waits for them, and re-layouts  3.05 us

commit v1 on v0

v1 whole, which is shorter than its diff:
```python
import functools
import math

import jax
import jax.numpy as jnp
from jax import lax
from jax.experimental import pallas as pl
from jax.experimental.pallas import tpu as pltpu
from jax.sharding import PartitionSpec as P

EPS = 1e-06
MESH = pl.DeviceIdType.MESH
LANES = 128
SAME = 640.0


def layer_kernel(
    cfg,
    x_ref,
    ids_ref,
    gain_ref,
    w_ref,
    scale_ref,
    wo_ref,
    bits_ref,
    off_ref,
    mixed_ref,
    codes_ref,
    ent_ref,
    wg,
    wog,
    xg,
    idg,
    normed,
    qs,
    ks,
    vs,
    ao,
    ag,
    part1,
    part2,
    local_sem,
    wz_s,
    wz_r,
    wx_s,
    wx_r,
    oz_s,
    oz_r,
    ox_s,
    ox_r,
    oy_s,
    oy_r,
    oc_s,
    oc_r,
    xy_s,
    xy_r,
    xc_s,
    xc_r,
    id_s,
    id_r,
    at_s,
    at_r,
    p1_s,
    p1_r,
    p2_s,
    p2_r,
):
    nz, nx, ny, nc = cfg["nz"], cfg["nx"], cfg["ny"], cfg["nc"]
    n = ny * nc
    ndp = nz * nx
    heads, channel = cfg["heads"], cfg["channel"]
    parts, quarters = cfg["parts"], cfg["quarters"]
    rows, width = x_ref.shape
    shard = w_ref.shape[0]
    cols = width // n
    pc = cols // parts
    sub = width // (nc * ny)
    seq_len = rows * n
    bits = bits_ref.shape[0]
    dp = lax.axis_index("dp")
    me = lax.axis_index("seq")
    z = dp // nx
    x = dp % nx
    y = me // nc
    core = me % nc

    def dp_at(zz, xx):
        return zz * nx + xx

    def seq_at(yy, cc):
        return yy * nc + cc

    def remote(src, dst, ss, rs, d, s):
        return pltpu.make_async_remote_copy(
            src_ref=src, dst_ref=dst, send_sem=ss, recv_sem=rs, device_id=(d, s), device_id_type=MESH
        )

    sends = []

    def go(make):
        make().start()
        sends.append(make)

    def arrive(slot, sem):
        remote(slot, slot, sem, sem, dp, me).wait_recv()

    def shard_rows(zz, xx):
        return pl.ds(pl.multiple_of(dp_at(zz, xx) * shard, shard), shard)

    def w_slot_of(h):
        return lambda zz, xx: wg.at[h, shard_rows(zz, xx), :]

    w_slots = [w_slot_of(h) for h in range(parts)]
    x_rows = rows // quarters

    def x_piece(member, q):
        return xg.at[member, pl.ds(q * x_rows, x_rows), :]

    def o_slot(zz, xx):
        return wog.at[core, :, shard_rows(zz, xx), :]

    def o_sub(yy, zz, xx):
        return wog.at[core, yy, shard_rows(zz, xx), :]

    lo = jnp.minimum(z, nz - 1 - z)

    def piece(i):
        near = z - (i + 1) // 2 if i % 2 else z + (i + 1) // 2
        far = jnp.where(z > nz - 1 - z, z - (i - lo), z + (i - lo))
        return jnp.where(i <= 2 * lo, near, far) if i else z

    line_sends = []

    def line_hops(slot, ss, rs, i):
        p = piece(i)
        here = slot(p, x)
        s_left, s_right = (ss.at[p], ss.at[p]) if i else (ss.at[nz], ss.at[nz + 1])
        left = remote(here, here, s_left, rs.at[p], dp_at(jnp.maximum(z - 1, 0), x), me)
        right = remote(here, here, s_right, rs.at[p], dp_at(jnp.minimum(z + 1, nz - 1), x), me)
        to_left = jnp.logical_and(p >= z, z > 0)
        to_right = jnp.logical_and(p <= z, z < nz - 1)
        return (to_left, left), (to_right, right)

    def line_start(slot, ss, rs, i):
        if nz == 1:
            return
        line_sends.append((slot, ss, rs, i))
        for wanted, hop in line_hops(slot, ss, rs, i):

            @pl.when(wanted)
            def _(hop=hop):
                hop.start()

    def cross(slot, ss, rs, i, k):
        p = piece(i)
        return remote(slot(p, x), slot(p, x), ss.at[p, k], rs.at[p, k], dp_at(z, (x + k) % nx), me)

    def across(slot, ss, rs, i):
        for k in range(1, nx):
            go(functools.partial(cross, slot, ss, rs, i, k))

    def share(src, key):
        def copy(k):
            here = src()
            return remote(here, here, oc_s.at[key, k], oc_r.at[key, k], dp, seq_at(y, (core + k) % nc))

        for k in range(1, nc):
            go(functools.partial(copy, k))

    def o_crossing(i, k, d):
        return o_sub((y - d + ny) % ny, piece(i), (x - k + nx) % nx)

    def o_over(i, k, d):
        p, s = piece(i), o_crossing(i, k, 0)
        return remote(s, s, oy_s.at[p, k, d], oy_r.at[p, k, d], dp, seq_at((y + d) % ny, core))

    def o_forward(i):
        line_start(o_slot, oz_s, oz_r, i)
        across(lambda zz, xx: o_sub(y, zz, xx), ox_s, ox_r, i)
        share(lambda: o_slot(piece(i), x), i)

    def o_line(i):
        arrive(o_slot(piece(i), x), oz_r.at[piece(i)])
        o_forward(i)

    def o_crossed(i):
        for k in range(1, nx):
            arrive(o_crossing(i, k, 0), ox_r.at[piece(i), k])
            for d in range(1, ny):
                go(functools.partial(o_over, i, k, d))
            share(functools.partial(o_crossing, i, k, 0), nz + (i * nx + k) * ny)

    def o_last(i):
        for k in range(1, nx):
            for d in range(1, ny):
                arrive(o_crossing(i, k, d), oy_r.at[piece(i), k, d])
                share(functools.partial(o_crossing, i, k, d), nz + (i * nx + k) * ny + d)

    def o_shared():
        for k in range(1, nc):
            other = (core - k + nc) % nc
            for i in range(nz):
                p = piece(i)
                s = wog.at[other, :, shard_rows(p, x), :]
                arrive(s, oc_r.at[i, k])
                for j in range(1, nx):
                    xx = (x - j + nx) % nx
                    for d in range(ny):
                        s = wog.at[other, (y - d + ny) % ny, shard_rows(p, xx), :]
                        arrive(s, oc_r.at[nz + (i * nx + j) * ny + d, k])

    own_w, own_o = [], []
    for h in range(parts):
        for part in range(3):
            own_w.append(
                pltpu.make_async_copy(
                    w_ref.at[:, pl.ds(pl.multiple_of(part * width + me * cols + h * pc, LANES), pc)],
                    wg.at[h, shard_rows(z, x), pl.ds(part * pc, pc)],
                    local_sem.at[h * 3 + part],
                )
            )
    base = 3 * parts
    own_x = pltpu.make_async_copy(x_ref, xg.at[me], local_sem.at[base])
    own_id = pltpu.make_async_copy(ids_ref, idg.at[me], local_sem.at[base + 1])
    for yy in range(ny):
        own_o.append(
            pltpu.make_async_copy(
                wo_ref.at[:, pl.ds(pl.multiple_of((core * ny + yy) * sub, LANES), sub)],
                o_sub(yy, z, x),
                local_sem.at[base + 2 + yy],
            )
        )
    for c in own_w + [own_x, own_id] + own_o:
        c.start()

    barrier = pltpu.get_barrier_semaphore()

    def greet(d, s):
        pl.semaphore_signal(barrier, inc=1, device_id=(d, s), device_id_type=MESH)

    for i in range(1, n):
        greet(dp, (me + i) % n)
    for k in range(1, nx):
        greet(dp_at(z, (x + k) % nx), me)

    @pl.when(z > 0)
    def _():
        greet(dp_at(z - 1, x), me)

    @pl.when(z < nz - 1)
    def _():
        greet(dp_at(z + 1, x), me)

    ends = jnp.where(z > 0, 1, 0) + jnp.where(z < nz - 1, 1, 0)
    pl.semaphore_wait(barrier, n - 1 + nx - 1 + ends)

    for c in own_w:
        c.wait()
    for h, slot in enumerate(w_slots):
        line_start(slot, wz_s.at[h], wz_r.at[h], 0)
        across(slot, wx_s.at[h], wx_r.at[h], 0)
    own_x.wait()
    for q in range(quarters):
        for i in range(1, ny):
            mine = x_piece(me, q)
            go(functools.partial(remote, mine, mine, xy_s.at[q, i], xy_r.at[q, i], dp, seq_at((y + i) % ny, core)))
    for k in range(1, nc):
        go(functools.partial(remote, xg.at[me], xg.at[me], xc_s.at[0, 0, k], xc_r.at[0, 0, k], dp, seq_at(y, (core + k) % nc)))
    own_id.wait()
    for i in range(1, n):
        go(functools.partial(remote, idg.at[me], idg.at[me], id_s.at[i], id_r.at[i], dp, (me + i) % n))

    gain = gain_ref[...]
    block = math.gcd(x_rows, 64)

    def norm_rows(member, q, count=1):
        start = pl.multiple_of(member * rows, rows)

        def body(b, _):
            r0 = pl.multiple_of(q * x_rows + b * block, block)
            wide = xg[member, pl.ds(r0, block), :].astype(jnp.float32)
            ms = jnp.mean(wide * wide, axis=-1, keepdims=True)
            out = (wide * lax.rsqrt(ms + EPS) * gain).astype(jnp.bfloat16)
            normed[pl.ds(start + r0, block), :] = out
            return 0

        lax.fori_loop(0, count * x_rows // block, body, 0)

    norm_rows(me, 0, quarters)
    for i in range(1, n):
        arrive(idg.at[(me - i + n) % n], id_r.at[i])
    lane_ids = lax.broadcasted_iota(jnp.int32, (rows, LANES), 1).astype(jnp.float32)
    for m in range(n):
        column = jnp.transpose(jnp.broadcast_to(idg[m].astype(jnp.float32), (LANES, rows)))
        hot = jnp.where(column == lane_ids, 1.0, 0.0)
        r = pl.ds(m * rows, rows)
        for h in range(parts):
            qs[h, r, pc:] = (hot * SAME).astype(jnp.bfloat16)
            ks[h, r, pc:] = hot.astype(jnp.bfloat16)
            vs[h, r, pc:] = jnp.ones((rows, pc), jnp.bfloat16)
    for k in range(1, nc):
        other = seq_at(y, (core - k + nc) % nc)
        arrive(xg.at[other], xc_r.at[0, 0, k])
        norm_rows(other, 0, quarters)

    def x_arrived(i, q):
        source = seq_at((y - i + ny) % ny, core)
        slot = x_piece(source, q)
        arrive(slot, xy_r.at[q, i])
        for k in range(1, nc):
            go(functools.partial(remote, slot, slot, xc_s.at[q, i, k], xc_r.at[q, i, k], dp, seq_at(y, (core + k) % nc)))
        norm_rows(source, q)

    def x_shared(i, q):
        for k in range(1, nc):
            other = seq_at((y - i + ny) % ny, (core - k + nc) % nc)
            arrive(x_piece(other, q), xc_r.at[q, i, k])
            norm_rows(other, q)

    def w_cross(i, h):
        across(w_slots[h], wx_s.at[h], wx_r.at[h], i)

    def w_arrived(i, h):
        arrive(w_slots[h](piece(i), x), wz_r.at[h, piece(i)])
        line_start(w_slots[h], wz_s.at[h], wz_r.at[h], i)
        if h == 0:
            w_cross(i, 0)
            for hh in range(1, parts):
                if i > 1:
                    w_cross(i - 1, hh)
        elif i == nz - 1:
            w_cross(i, h)

    events = []
    for i in range(1, nz):
        for h in range(parts):
            events.append((((i - 1) * parts + h + 1) * shard * 3 * pc, 0, i, h))
    for i in range(1, ny):
        for q in range(quarters):
            events.append((((i - 1) * quarters + q + 1) * x_rows * width, 1, i, q))
    waiting = []
    for _, stream, i, j in sorted(events):
        if stream == 0:
            w_arrived(i, j)
        else:
            x_arrived(i, j)
            waiting.append((i, j))
            if len(waiting) > 1:
                x_shared(*waiting.pop(0))
    for c in own_o:
        c.wait()
    o_forward(0)
    for late in waiting:
        x_shared(*late)

    row_block = 256
    blocks = seq_len // row_block

    def group_of(shape, dim):
        return lax.div(lax.broadcasted_iota(jnp.int32, shape, dim), jnp.int32(channel))

    pair = (2 * pc, 2 * pc)
    same_head = jnp.where(group_of(pair, 0) == group_of(pair, 1), 1.0, 0.0).astype(jnp.bfloat16)
    part_heads = pc // channel

    def project(h):
        scale_row = jnp.ones((1, 2 * pc), jnp.float32)
        for g in range(part_heads):
            value = scale_ref[me * heads + h * part_heads + g] / math.sqrt(channel)
            scale_row = jnp.where(group_of((1, 2 * pc), 1) == g, value, scale_row)
        for i in range(nz):
            for k in range(1, nx):
                arrive(w_slots[h](piece(i), (x - k + nx) % nx), wx_r.at[h, piece(i), k])

        def body(b, _):
            r = pl.ds(pl.multiple_of(b * row_block, row_block), row_block)
            joined = jnp.dot(normed[r, :], wg[h], preferred_element_type=jnp.float32).astype(jnp.bfloat16)
            qk = joined[:, : 2 * pc].astype(jnp.float32)
            square = qk * qk
            high = square.astype(jnp.bfloat16)
            low = (square - high.astype(jnp.float32)).astype(jnp.bfloat16)
            total = jnp.dot(high, same_head, preferred_element_type=jnp.float32) + jnp.dot(
                low, same_head, preferred_element_type=jnp.float32
            )
            qk = (qk * lax.rsqrt(total / channel + EPS) * scale_row).astype(jnp.bfloat16)
            qs[h, r, :pc] = qk[:, :pc]
            ks[h, r, :pc] = qk[:, pc:]
            vs[h, r, :pc] = joined[:, 2 * pc :]
            return 0

        lax.fori_loop(0, blocks, body, 0)

    q_block = cfg["q_block"]
    lane_head = group_of((q_block, pc), 1)

    def stage_target(t, sign):
        dy = (t // nc + 1) % ny
        dc = (t + 1) % nc
        if sign > 0:
            return seq_at((y + dy) % ny, (core + dc) % nc)
        return seq_at((y - dy + ny) % ny, (core - dc + nc) % nc)

    def a2a(h, t):
        j = stage_target(t, 1)
        return remote(ao.at[h, j], ag.at[h, me], at_s.at[h, t], at_r.at[h, t], dp, j)

    def attend(h, chores):
        def stage(t, _):
            j = stage_target(t, 1)
            for part in range(rows // q_block):
                r = pl.ds(pl.multiple_of(j * rows + part * q_block, q_block), q_block)
                qb = qs[h, r, :]
                out = jnp.zeros((q_block, pc), jnp.float32)
                for g in range(part_heads):
                    mine = lane_head == g
                    qh = jnp.concatenate([jnp.where(mine, qb[:, :pc], jnp.zeros_like(qb[:, :pc])), qb[:, pc:]], axis=1)
                    s = lax.dot_general(qh, ks[h], (((1,), (1,)), ((), ())), preferred_element_type=jnp.float32)
                    p = jnp.exp(s - jnp.max(s, axis=-1, keepdims=True))
                    o = jnp.dot(p.astype(jnp.bfloat16), vs[h], preferred_element_type=jnp.float32)
                    out = jnp.where(mine, o[:, :pc] / o[:, pc:], out)
                ao[h, j, pl.ds(part * q_block, q_block), :] = out.astype(jnp.bfloat16)

            @pl.when(t < n - 1)
            def _():
                a2a(h, t).start()

            for at in sorted(set(chores)):

                @pl.when(t == at)
                def _(at=at):
                    for c in chores[at]:
                        c()

            return 0

        lax.fori_loop(0, n, stage, 0)

    todo = []
    for i in range(1, nz + 2):
        if i < nz:
            todo.append(functools.partial(o_line, i))
        if 0 <= i - 2 < nz:
            todo.append(functools.partial(o_crossed, i - 2))
        if 0 <= i - 3 < nz:
            todo.append(functools.partial(o_last, i - 3))
    todo += [functools.partial(o_last, i) for i in range(max(0, nz - 1), nz)]

    for h in range(parts):
        project(h)
        chores = {}
        if h == parts - 1:
            for t in range(n):
                chores[t] = [todo.pop(0) for _ in range(min(len(todo), 1))]
        else:
            chores[n - 1] = [todo.pop(0)]
        attend(h, chores)
    for c in todo:
        c()
    o_shared()

    for h in range(parts):
        for t in range(n - 1):
            arrive(ag.at[h, stage_target(t, -1)], at_r.at[h, t])
        ag[h, me] = ao[h, me]

    attention = jnp.concatenate([ag[h, m] for m in range(n) for h in range(parts)], axis=1)
    for g in range(nc * ny):
        lanes = slice(g * sub, (g + 1) * sub)
        prod = jnp.dot(attention, wog[g // ny, g % ny], preferred_element_type=jnp.float32)
        mixed_ref[:, lanes] = (xg[me, :, lanes].astype(jnp.float32) + prod).astype(jnp.bfloat16)

    logits = lax.dot_general(
        bits_ref[...], mixed_ref[...], (((1,), (1,)), ((), ())), preferred_element_type=jnp.float32
    )
    eye = lax.broadcasted_iota(jnp.int32, (bits, bits), 0) == lax.broadcasted_iota(
        jnp.int32, (bits, bits), 1
    )
    offset = jnp.sum(jnp.where(eye, off_ref[...], 0.0), axis=1, keepdims=True)
    probs = jax.nn.sigmoid(4.0 * (logits + offset))
    lanes_eye = lax.broadcasted_iota(jnp.int32, (bits, LANES), 0) == lax.broadcasted_iota(
        jnp.int32, (bits, LANES), 1
    )
    own_sums = jnp.sum(probs, axis=1, keepdims=True)
    part1[me, :, :] = jnp.sum(jnp.where(lanes_eye, own_sums, 0.0), axis=0, keepdims=True)
    for i in range(1, n):
        go(functools.partial(remote, part1.at[me], part1.at[me], p1_s.at[i], p1_r.at[i], dp, (me + i) % n))
    for i in range(1, n):
        arrive(part1.at[(me - i + n) % n], p1_r.at[i])
    pack = part1[0]
    for m in range(1, n):
        pack = pack + part1[m]
    part2[dp, :, :] = pack
    for i in range(1, ndp):
        go(functools.partial(remote, part2.at[dp], part2.at[dp], p2_s.at[i], p2_r.at[i], (dp + i) % ndp, me))
    for i in range(1, ndp):
        arrive(part2.at[(dp - i + ndp) % ndp], p2_r.at[i])
    total = part2[0]
    for m in range(1, ndp):
        total = total + part2[m]
    marginal = total / (seq_len * ndp)
    line = marginal[:, :bits]
    ent_ref[...] = -(line * jnp.log(line) + (1.0 - line) * jnp.log(1.0 - line))
    codes = probs - jnp.sum(jnp.where(lanes_eye, marginal, 0.0), axis=1, keepdims=True)
    for b in range(bits):
        codes_ref[b] = codes[b : b + 1, :]

    for make in sends:
        make().wait_send()
    for h in range(parts):
        for t in range(n - 1):
            a2a(h, t).wait_send()
    for hops in line_sends:
        for wanted, hop in line_hops(*hops):

            @pl.when(wanted)
            def _(hop=hop):
                hop.wait_send()


def on_device(
    cfg,
    residual_tiles,
    picture_label_tile,
    prenorm_multiplier,
    triple_projector,
    logit_scaling,
    final_projector,
    binarizer_projector,
    binarizer_offset,
):
    nz, nx, ny, nc = cfg["nz"], cfg["nx"], cfg["ny"], cfg["nc"]
    n, ndp = ny * nc, nz * nx
    _, rows, width = residual_tiles.shape
    heads_all = logit_scaling.shape[0]
    bits = binarizer_projector.shape[1]
    cols = width // n
    shard = triple_projector.shape[0]
    seq_len = rows * n
    parts = cols // LANES if cols % LANES == 0 else 1
    pc, sub = cols // parts, width // (nc * ny)
    quarters = 4 if rows % 128 == 0 else 1
    cfg = dict(
        cfg,
        heads=heads_all // n,
        channel=width // heads_all,
        q_block=min(256, rows),
        parts=parts,
        quarters=quarters,
    )
    dma = pltpu.SemaphoreType.DMA
    vmem, hbm = pl.BlockSpec(memory_space=pltpu.VMEM), pl.BlockSpec(memory_space=pl.ANY)
    smem = pl.BlockSpec(memory_space=pltpu.SMEM)
    bf16, f32 = jnp.bfloat16, jnp.float32
    keys = nz + nz * nx * ny + nx * ny
    mixed, codes, ent = pl.pallas_call(
        functools.partial(layer_kernel, cfg),
        out_shape=(
            pltpu.VMEM((rows, width), bf16),
            pltpu.VMEM((bits, 1, rows), f32),
            pltpu.VMEM((1, bits), f32),
        ),
        in_specs=[hbm, vmem, vmem, hbm, smem, hbm, vmem, vmem],
        out_specs=(vmem, vmem, vmem),
        scratch_shapes=[
            pltpu.VMEM((parts, width, 3 * pc), bf16),
            pltpu.VMEM((nc, ny, width, sub), bf16),
            pltpu.VMEM((n, rows, width), bf16),
            pltpu.VMEM((n, 1, rows), jnp.int32),
            pltpu.VMEM((seq_len, width), bf16),
            pltpu.VMEM((parts, seq_len, pc + LANES), bf16),
            pltpu.VMEM((parts, seq_len, pc + LANES), bf16),
            pltpu.VMEM((parts, seq_len, 2 * pc), bf16),
            pltpu.VMEM((parts, n, rows, pc), bf16),
            pltpu.VMEM((parts, n, rows, pc), bf16),
            pltpu.VMEM((n, 1, LANES), f32),
            pltpu.VMEM((ndp, 1, LANES), f32),
            dma((3 * parts + 2 + ny,)),
            dma((parts, nz + 2)),
            dma((parts, nz)),
            dma((parts, nz, nx)),
            dma((parts, nz, nx)),
            dma((nz + 2,)),
            dma((nz,)),
            dma((nz, nx)),
            dma((nz, nx)),
            dma((nz, nx, ny)),
            dma((nz, nx, ny)),
            dma((keys, nc)),
            dma((keys, nc)),
            dma((quarters, ny)),
            dma((quarters, ny)),
            dma((quarters, ny, nc)),
            dma((quarters, ny, nc)),
            dma((n,)),
            dma((n,)),
            dma((parts, n)),
            dma((parts, n)),
            dma((n,)),
            dma((n,)),
            dma((ndp,)),
            dma((ndp,)),
        ],
        compiler_params=pltpu.CompilerParams(
            collective_id=0, has_side_effects=True, vmem_limit_bytes=56 * 1024 * 1024
        ),
        name="layer",
    )(
        residual_tiles[0],
        picture_label_tile,
        prenorm_multiplier[None],
        triple_projector,
        logit_scaling,
        final_projector,
        binarizer_projector.T,
        binarizer_offset[None],
    )
    return mixed[None], jnp.swapaxes(codes, 0, 1), ent[0]


def solution(mesh):
    ndp, n = mesh.shape["dp"], mesh.shape["seq"]
    nx = math.isqrt(ndp // 2)
    if nx < 1 or ndp % nx:
        nx = 1
    nc = 2 if n % 2 == 0 else 1
    cfg = {"nz": ndp // nx, "nx": nx, "ny": n // nc, "nc": nc}
    return jax.shard_map(
        functools.partial(on_device, cfg),
        mesh=mesh,
        in_specs=(
            P("dp", "seq", None),
            P("dp", "seq"),
            P(),
            P("dp", None),
            P(),
            P("dp", None),
            P(),
            P(),
        ),
        out_specs=(P("dp", "seq", None), P("dp", None, "seq"), P()),
        check_vma=False,
    )
```

time: 59 us -> 69.4 us (1.18)
  Pallas kernels: 55.1 us -> 66.7 us
  local copies, waits for them, and re-layouts: 3.05 us -> 1.91 us
    pallas_call x1, Pallas kernels: 55.1 us -> 66.7 us  [on_device(): pl.pallas_call(functools.partial(layer_kernel, cfg), out_shape=(pltpu.VME...]
    unnamed x7 -> x3, local copies, waits for them, and re-layouts: 3.05 us -> 1.91 us
where the time goes in v1:
time: 69.4 us; the launch traced here: 69.2 us
  Pallas kernels  66.7 us (96%)
  local copies, waits for them, and re-layouts  1.91 us (3%)
    pallas_call x1, Pallas kernels, on_device(): pl.pallas_call(functools.partial(layer_kernel, cfg), out_shape=(pltpu.VME...  66.7 us
    unnamed x3, local copies, waits for them, and re-layouts  1.91 us

profile of v1, /device:TPU:0, one launch (start us, length us, event | category | flops | bytes accessed | tf_op | source)
XLA Modules:
  0.0 69.2 jit_solution(16585208859321954412)
XLA Ops:
  0.6 66.7 %layer.1 = (bf16[256,1024]{1,0:T(8,128)(2,1)S(1)}, f32[18,1,256]{2,1,0:T(1,128)S(1)}, f32[1,18]{1,0:T(1,128)S(1)}) custom-call(bf16[256,1024]{1,0:T(8,128)(2,1)} %bitcast.10, s32[1,256]{1,0:T(1,128)} %ids_ref.1, f32[1,1024]{1,0:T(1,128)} %bitcast.12, bf16[128,3072]{1,0:T(8,128)(2,1)} %w_ref.1, f32[16]{0:T(128)} %scale_ref.1, bf16[128,1024]{1,0:T(8,128)(2,1)} %wo_ref.1, ...), custom_call_target="tpu_custom_call" | custom-call | tf_op jit(solution)/shard_map/layer/pallas_call | solution.py:555
  67.3 0.8 %copy.14 = bf16[1,256,1024]{2,1,0:T(8,128)(2,1)} copy(bf16[1,256,1024]{2,1,0:T(8,128)(2,1)S(1)} %bitcast.7) | data formatting | bytes 1048576
  68.1 0.6 copy.15
  68.7 0.5 copy.16

commit v2 on v1

v2 whole, which is shorter than its diff:
```python
import functools
import math

import jax
import jax.numpy as jnp
from jax import lax
from jax.experimental import pallas as pl
from jax.experimental.pallas import tpu as pltpu
from jax.sharding import PartitionSpec as P

EPS = 1e-06
MESH = pl.DeviceIdType.MESH
LANES = 128
SAME = 640.0


def layer_kernel(
    cfg,
    x_ref,
    ids_ref,
    gain_hbm,
    w_ref,
    scale_hbm,
    wo_ref,
    bits_hbm,
    off_hbm,
    mixed_ref,
    codes_ref,
    ent_ref,
    wg,
    wog,
    xg,
    idg,
    normed,
    qs,
    ks,
    vs,
    ao,
    ag,
    stats,
    gain_ref,
    scale_ref,
    bits_ref,
    off_ref,
    local_sem,
    wz_s,
    wz_r,
    wx_s,
    wx_r,
    oz_s,
    oz_r,
    ox_s,
    ox_r,
    oy_s,
    oy_r,
    oc_s,
    oc_r,
    xy_s,
    xy_r,
    xc_s,
    own_r,
    xc_r,
    id_s,
    id_r,
    at_s,
    at_r,
    st_s,
    st_r,
):
    nz, nx, ny, nc = cfg["nz"], cfg["nx"], cfg["ny"], cfg["nc"]
    n = ny * nc
    ndp = nz * nx
    heads, channel = cfg["heads"], cfg["channel"]
    parts, quarters = cfg["parts"], cfg["quarters"]
    rows, width = x_ref.shape
    shard = w_ref.shape[0]
    cols = width // n
    pc = cols // parts
    sub = width // (nc * ny)
    seq_len = rows * n
    bits = bits_ref.shape[0]
    dp = lax.axis_index("dp")
    me = lax.axis_index("seq")
    z = dp // nx
    x = dp % nx
    y = me // nc
    core = me % nc

    def dp_at(zz, xx):
        return zz * nx + xx

    def seq_at(yy, cc):
        return yy * nc + cc

    def remote(src, dst, ss, rs, d, s):
        return pltpu.make_async_remote_copy(
            src_ref=src, dst_ref=dst, send_sem=ss, recv_sem=rs, device_id=(d, s), device_id_type=MESH
        )

    def arrive(slot, sem):
        remote(slot, slot, sem, sem, dp, me).wait_recv()

    def left(slot, sem):
        remote(slot, slot, sem, sem, dp, me).wait_send()

    def shard_rows(zz, xx):
        return pl.ds(pl.multiple_of(dp_at(zz, xx) * shard, shard), shard)

    def w_slot_of(h):
        return lambda zz, xx: wg.at[h, shard_rows(zz, xx), :]

    w_slots = [w_slot_of(h) for h in range(parts)]
    x_rows = rows // quarters

    def x_piece(member, q):
        return xg.at[member, pl.ds(q * x_rows, x_rows), :]

    def o_slot(zz, xx):
        return wog.at[core, :, shard_rows(zz, xx), :]

    def o_sub(yy, zz, xx):
        return wog.at[core, yy, shard_rows(zz, xx), :]

    lo = jnp.minimum(z, nz - 1 - z)

    def piece(i):
        near = z - (i + 1) // 2 if i % 2 else z + (i + 1) // 2
        far = jnp.where(z > nz - 1 - z, z - (i - lo), z + (i - lo))
        return jnp.where(i <= 2 * lo, near, far) if i else z

    def line_start(slot, ss, rs, i, when=True):
        if nz == 1:
            return
        p = piece(i)
        here = slot(p, x)
        to_left = remote(here, here, ss.at[0], rs.at[p], dp_at(jnp.maximum(z - 1, 0), x), me)
        to_right = remote(here, here, ss.at[1], rs.at[p], dp_at(jnp.minimum(z + 1, nz - 1), x), me)
        for wanted, hop in (
            (jnp.logical_and(p >= z, z > 0), to_left),
            (jnp.logical_and(p <= z, z < nz - 1), to_right),
        ):

            @pl.when(wanted if when is True else jnp.logical_and(wanted, when))
            def _(hop=hop):
                hop.start()

    def line_left(block, ss):
        for zz in range(nz if nz > 1 else 0):

            @pl.when(z == zz)
            def _(zz=zz):
                if zz > 0:
                    left(block(nz - zz), ss.at[0])
                if zz < nz - 1:
                    left(block(zz + 1), ss.at[1])

    def across(slot, ss, rs, i):
        p = piece(i)
        for k in range(1, nx):
            remote(slot(p, x), slot(p, x), ss, rs(k), dp_at(z, (x + k) % nx), me).start()

    def share(here):
        for k in range(1, nc):
            remote(here, here, oc_s.at[k], oc_r.at[k], dp, seq_at(y, (core + k) % nc)).start()

    def whole(i):
        return i >= nz - 2 or ny == 1

    def o_crossing(i, k, d):
        p, xx = piece(i), (x - k + nx) % nx
        return o_slot(p, xx) if whole(i) else o_sub((y - d + ny) % ny, p, xx)

    def o_line_start(i, when=True):
        line_start(o_slot, oz_s, oz_r, i, when)

    def o_cross(i):
        slot = o_slot if whole(i) else lambda zz, xx: o_sub(y, zz, xx)
        across(slot, ox_s.at[int(whole(i))], lambda k: ox_r.at[i, k], i)

    def o_line(i):
        p = piece(i)
        arrive(o_slot(p, x), oz_r.at[p])
        o_line_start(i)
        o_cross(i)
        share(o_slot(p, x))

    def o_crossed(i):
        for k in range(1, nx):
            here = o_crossing(i, k, 0)
            arrive(here, ox_r.at[i, k])
            if not whole(i):
                for d in range(1, ny):
                    remote(
                        here, here, oy_s.at[d], oy_r.at[i, k, d], dp, seq_at((y + d) % ny, core)
                    ).start()
            share(here)

    def o_last(i):
        for k in range(1, nx):
            for d in range(1, 1 if whole(i) else ny):
                arrive(o_crossing(i, k, d), oy_r.at[i, k, d])
                share(o_crossing(i, k, d))

    def o_shared():
        for k in range(1, nc):
            arrive(wog.at[(core - k + nc) % nc], oc_r.at[k])

    own_w, own_o = [], []
    for h in range(parts):
        for part in range(3):
            own_w.append(
                pltpu.make_async_copy(
                    w_ref.at[:, pl.ds(pl.multiple_of(part * width + me * cols + h * pc, LANES), pc)],
                    wg.at[h, shard_rows(z, x), pl.ds(part * pc, pc)],
                    local_sem.at[0],
                )
            )
    own_x = pltpu.make_async_copy(x_ref, xg.at[me], local_sem.at[1])
    own_id = pltpu.make_async_copy(ids_ref, idg.at[me], local_sem.at[2])
    for yy in range(ny):
        own_o.append(
            pltpu.make_async_copy(
                wo_ref.at[:, pl.ds(pl.multiple_of((core * ny + yy) * sub, LANES), sub)],
                o_sub(yy, z, x),
                local_sem.at[3],
            )
        )
    own_small = [
        pltpu.make_async_copy(src, dst, local_sem.at[4 + i])
        for i, (src, dst) in enumerate(
            ((gain_hbm, gain_ref), (scale_hbm, scale_ref), (bits_hbm, bits_ref), (off_hbm, off_ref))
        )
    ]
    for c in own_w + [own_id, own_x] + own_small + own_o:
        c.start()

    barrier = pltpu.get_barrier_semaphore()

    def greet(d, s):
        pl.semaphore_signal(barrier, inc=1, device_id=(d, s), device_id_type=MESH)

    for i in range(1, n):
        greet(dp, (me + i) % n)
    for k in range(1, nx):
        greet(dp_at(z, (x + k) % nx), me)

    @pl.when(z > 0)
    def _():
        greet(dp_at(z - 1, x), me)

    @pl.when(z < nz - 1)
    def _():
        greet(dp_at(z + 1, x), me)

    ends = jnp.where(z > 0, 1, 0) + jnp.where(z < nz - 1, 1, 0)
    pl.semaphore_wait(barrier, n - 1 + nx - 1 + ends)

    own_block = wg.at[:, shard_rows(z, x), :]
    pltpu.make_async_copy(own_block, own_block, local_sem.at[0]).wait()

    def w_forward(i, h):
        line_start(w_slots[h], wz_s, wz_r.at[h], i)
        across(w_slots[h], wx_s.at[h], lambda k: wx_r.at[h], i)

    for h in range(parts):
        w_forward(0, h)
    own_id.wait()
    for i in range(1, n):
        remote(idg.at[me], idg.at[me], id_s, id_r, dp, (me + i) % n).start()
    own_x.wait()
    for q in range(quarters):
        for i in range(1, ny):
            mine = x_piece(me, q)
            remote(mine, mine, xy_s.at[i], xy_r.at[q, i], dp, seq_at((y + i) % ny, core)).start()
    for k in range(1, nc):
        remote(xg.at[me], xg.at[me], xc_s.at[k], own_r.at[k], dp, seq_at(y, (core + k) % nc)).start()

    for c in own_small:
        c.wait()
    own_block = o_slot(z, x)
    pltpu.make_async_copy(own_block, own_block, local_sem.at[3]).wait()
    o_line_start(0, lo == 0)

    gain = gain_ref[...]
    block = math.gcd(x_rows, 64)

    def norm_rows(member, q, count=1):
        start = pl.multiple_of(member * rows, rows)

        def body(b, _):
            r0 = pl.multiple_of(q * x_rows + b * block, block)
            wide = xg[member, pl.ds(r0, block), :].astype(jnp.float32)
            ms = jnp.mean(wide * wide, axis=-1, keepdims=True)
            out = (wide * lax.rsqrt(ms + EPS) * gain).astype(jnp.bfloat16)
            normed[pl.ds(start + r0, block), :] = out
            return 0

        lax.fori_loop(0, count * x_rows // block, body, 0)

    norm_rows(me, 0, quarters)
    arrive(idg.at[pl.ds(0, n - 1)], id_r)
    lane_ids = lax.broadcasted_iota(jnp.int32, (rows, LANES), 1).astype(jnp.float32)
    for m in range(n):
        column = jnp.transpose(jnp.broadcast_to(idg[m].astype(jnp.float32), (LANES, rows)))
        hot = jnp.where(column == lane_ids, 1.0, 0.0)
        r = pl.ds(m * rows, rows)
        for h in range(parts):
            qs[h, r, pc:] = (hot * SAME).astype(jnp.bfloat16)
            ks[h, r, pc:] = hot.astype(jnp.bfloat16)
            vs[h, r, pc:] = jnp.ones((rows, pc), jnp.bfloat16)
    for k in range(1, nc):
        other = seq_at(y, (core - k + nc) % nc)
        arrive(xg.at[other], own_r.at[k])
        norm_rows(other, 0, quarters)

    def x_arrived(i, q):
        source = seq_at((y - i + ny) % ny, core)
        slot = x_piece(source, q)
        arrive(slot, xy_r.at[q, i])
        for k in range(1, nc):
            remote(slot, slot, xc_s.at[k], xc_r.at[q, i - 1, k], dp, seq_at(y, (core + k) % nc)).start()
        norm_rows(source, q)

    def x_shared(i, q):
        for k in range(1, nc):
            other = seq_at((y - i + ny) % ny, (core - k + nc) % nc)
            arrive(x_piece(other, q), xc_r.at[q, i - 1, k])
            norm_rows(other, q)

    def w_arrived(i, h):
        arrive(w_slots[h](piece(i), x), wz_r.at[h, piece(i)])
        w_forward(i, h)

    events = []
    for i in range(1, nz):
        for h in range(parts):
            events.append((((i - 1) * parts + h + 1) * shard * 3 * pc, 0, i, h))
    for i in range(1, ny):
        for q in range(quarters):
            events.append((((i - 1) * quarters + q + 1) * x_rows * width, 1, i, q))
    waiting = []
    for _, stream, i, j in sorted(events):
        if stream == 0:
            w_arrived(i, j)
        else:
            x_arrived(i, j)
            waiting.append((i, j))
            if len(waiting) > 1:
                x_shared(*waiting.pop(0))
    o_line_start(0, lo > 0)
    o_cross(0)
    share(o_slot(z, x))
    for late in waiting:
        x_shared(*late)

    row_block = 256
    blocks = seq_len // row_block

    def group_of(shape, dim):
        return lax.div(lax.broadcasted_iota(jnp.int32, shape, dim), jnp.int32(channel))

    pair = (2 * pc, 2 * pc)
    same_head = jnp.where(group_of(pair, 0) == group_of(pair, 1), 1.0, 0.0).astype(jnp.bfloat16)
    part_heads = pc // channel

    def project(h):
        scale_row = jnp.ones((1, 2 * pc), jnp.float32)
        for g in range(part_heads):
            value = scale_ref[me * heads + h * part_heads + g] / math.sqrt(channel)
            scale_row = jnp.where(group_of((1, 2 * pc), 1) == g, value, scale_row)
        if nx > 1:
            arrive(wg.at[h, pl.ds(0, nz * (nx - 1) * shard), :], wx_r.at[h])

        for b in range(blocks):
            r = pl.ds(b * row_block, row_block)
            joined = jnp.dot(normed[r, :], wg[h], preferred_element_type=jnp.float32).astype(jnp.bfloat16)
            qk = joined[:, : 2 * pc].astype(jnp.float32)
            square = qk * qk
            high = square.astype(jnp.bfloat16)
            low = (square - high.astype(jnp.float32)).astype(jnp.bfloat16)
            total = jnp.dot(high, same_head, preferred_element_type=jnp.float32) + jnp.dot(
                low, same_head, preferred_element_type=jnp.float32
            )
            qk = (qk * lax.rsqrt(total / channel + EPS) * scale_row).astype(jnp.bfloat16)
            qs[h, r, :pc] = qk[:, :pc]
            ks[h, r, :pc] = qk[:, pc:]
            vs[h, r, :pc] = joined[:, 2 * pc :]

    q_block = cfg["q_block"]
    lane_head = group_of((q_block, pc), 1)

    def stage_target(t, sign):
        dy = (t // nc + 1) % ny
        dc = (t + 1) % nc
        if sign > 0:
            return seq_at((y + dy) % ny, (core + dc) % nc)
        return seq_at((y - dy + ny) % ny, (core - dc + nc) % nc)

    def a2a(h, t):
        j = stage_target(t, 1)
        return remote(ao.at[h, j], ag.at[h, me], at_s.at[h], at_r.at[h], dp, j)

    def attend(h, stages):
        for t in stages:
            j = stage_target(t, 1)
            for part in range(rows // q_block):
                r = pl.ds(pl.multiple_of(j * rows + part * q_block, q_block), q_block)
                qb = qs[h, r, :]
                out = jnp.zeros((q_block, pc), jnp.float32)
                for g in range(part_heads):
                    mine = lane_head == g
                    qh = jnp.concatenate([jnp.where(mine, qb[:, :pc], jnp.zeros_like(qb[:, :pc])), qb[:, pc:]], axis=1)
                    s = lax.dot_general(qh, ks[h], (((1,), (1,)), ((), ())), preferred_element_type=jnp.float32)
                    p = jnp.exp(s - jnp.max(s, axis=-1, keepdims=True))
                    o = jnp.dot(p.astype(jnp.bfloat16), vs[h], preferred_element_type=jnp.float32)
                    out = jnp.where(mine, o[:, :pc] / o[:, pc:], out)
                ao[h, j, pl.ds(part * q_block, q_block), :] = out.astype(jnp.bfloat16)
        for t in stages:
            if t < n - 1:
                a2a(h, t).start()

    for i in range(1, nz - 1):
        o_line(i)
    for h in range(parts):
        project(h)
        if h < parts - 1:
            attend(h, range(n))
            if h == 0 and nz > 1:
                o_line(nz - 1)
        else:
            o_crossed(0)
            attend(h, range(n // 2))
            if parts == 1 and nz > 1:
                o_line(nz - 1)
            if nz > 1:
                o_crossed(1)
            attend(h, range(n // 2, n))
    for i in range(2, nz):
        o_last(i - 2)
        o_crossed(i)
    for i in range(max(0, nz - 2), nz):
        o_last(i)
    o_shared()

    for h in range(parts):
        arrive(ag.at[h, pl.ds(0, n - 1)], at_r.at[h])
        ag[h, me] = ao[h, me]

    attention = jnp.concatenate([ag[h, m] for m in range(n) for h in range(parts)], axis=1)
    for g in range(nc * ny):
        lanes = slice(g * sub, (g + 1) * sub)
        prod = jnp.dot(attention, wog[g // ny, g % ny], preferred_element_type=jnp.float32)
        mixed_ref[:, lanes] = (xg[me, :, lanes].astype(jnp.float32) + prod).astype(jnp.bfloat16)

    logits = lax.dot_general(
        bits_ref[...], mixed_ref[...], (((1,), (1,)), ((), ())), preferred_element_type=jnp.float32
    )
    eye = lax.broadcasted_iota(jnp.int32, (bits, bits), 0) == lax.broadcasted_iota(
        jnp.int32, (bits, bits), 1
    )
    offset = jnp.sum(jnp.where(eye, off_ref[...], 0.0), axis=1, keepdims=True)
    probs = jax.nn.sigmoid(4.0 * (logits + offset))
    lanes_eye = lax.broadcasted_iota(jnp.int32, (bits, LANES), 0) == lax.broadcasted_iota(
        jnp.int32, (bits, LANES), 1
    )
    own_sums = jnp.sum(probs, axis=1, keepdims=True)
    count = n * ndp
    mine = dp * n + me
    stats[mine, :, :] = jnp.sum(jnp.where(lanes_eye, own_sums, 0.0), axis=0, keepdims=True)

    def tell(i, _):
        t = (mine + i) % count
        remote(stats.at[mine], stats.at[mine], st_s, st_r, t // n, t % n).start()
        return 0

    lax.fori_loop(1, count, tell, 0)
    others = stats.at[pl.ds(0, count - 1)]
    arrive(others, st_r)
    total = jnp.sum(stats[...], axis=0)
    marginal = total / (seq_len * ndp)
    line = marginal[:, :bits]
    ent_ref[...] = -(line * jnp.log(line) + (1.0 - line) * jnp.log(1.0 - line))
    codes = probs - jnp.sum(jnp.where(lanes_eye, marginal, 0.0), axis=1, keepdims=True)
    for b in range(bits):
        codes_ref[b] = codes[b : b + 1, :]

    left(others, st_s)
    line_left(lambda m: wg.at[:, pl.ds(0, m * shard), :], wz_s)
    line_left(lambda m: wog.at[0, :, pl.ds(0, m * shard), :], oz_s)
    halves = [i for i in range(nz) if not whole(i)]
    if nx > 1:
        for h in range(parts):
            left(wg.at[h, pl.ds(0, nz * (nx - 1) * shard), :], wx_s.at[h])
        if halves:
            block = wog.at[0, 0, pl.ds(0, len(halves) * (nx - 1) * shard), :]
            left(block, ox_s.at[0])
            for d in range(1, ny):
                left(block, oy_s.at[d])
        if len(halves) < nz:
            left(wog.at[0, :, pl.ds(0, (nz - len(halves)) * (nx - 1) * shard), :], ox_s.at[1])
    for k in range(1, nc):
        left(wog.at[core], oc_s.at[k])
        left(xg.at[pl.ds(0, ny)], xc_s.at[k])
    for i in range(1, ny):
        left(xg.at[me], xy_s.at[i])
    left(idg.at[pl.ds(0, n - 1)], id_s)
    for h in range(parts):
        left(ag.at[h, pl.ds(0, n - 1)], at_s.at[h])


def put_kernel(mixed_ref, codes_ref, ent_ref, mixed_out, codes_out, ent_out, sems):
    pairs = ((mixed_ref, mixed_out), (codes_ref, codes_out), (ent_ref, ent_out))
    copies = [pltpu.make_async_copy(src, dst, sems.at[i]) for i, (src, dst) in enumerate(pairs)]
    for c in copies:
        c.start()
    for c in copies:
        c.wait()


def on_device(
    cfg,
    residual_tiles,
    picture_label_tile,
    prenorm_multiplier,
    triple_projector,
    logit_scaling,
    final_projector,
    binarizer_projector,
    binarizer_offset,
):
    nz, nx, ny, nc = cfg["nz"], cfg["nx"], cfg["ny"], cfg["nc"]
    n, ndp = ny * nc, nz * nx
    _, rows, width = residual_tiles.shape
    heads_all = logit_scaling.shape[0]
    bits = binarizer_projector.shape[1]
    cols = width // n
    shard = triple_projector.shape[0]
    seq_len = rows * n
    parts = cols // LANES if cols % LANES == 0 else 1
    pc, sub = cols // parts, width // (nc * ny)
    quarters = 4 if rows % 128 == 0 else 1
    cfg = dict(
        cfg,
        heads=heads_all // n,
        channel=width // heads_all,
        q_block=min(256, rows),
        parts=parts,
        quarters=quarters,
    )
    dma = pltpu.SemaphoreType.DMA
    vmem, hbm = pl.BlockSpec(memory_space=pltpu.VMEM), pl.BlockSpec(memory_space=pl.ANY)
    bf16, f32 = jnp.bfloat16, jnp.float32
    mixed, codes, ent = pl.pallas_call(
        functools.partial(layer_kernel, cfg),
        out_shape=(
            pltpu.VMEM((rows, width), bf16),
            pltpu.VMEM((bits, 1, rows), f32),
            pltpu.VMEM((1, bits), f32),
        ),
        in_specs=[hbm] * 8,
        out_specs=(vmem, vmem, vmem),
        scratch_shapes=[
            pltpu.VMEM((parts, width, 3 * pc), bf16),
            pltpu.VMEM((nc, ny, width, sub), bf16),
            pltpu.VMEM((n, rows, width), bf16),
            pltpu.VMEM((n, 1, rows), jnp.int32),
            pltpu.VMEM((seq_len, width), bf16),
            pltpu.VMEM((parts, seq_len, pc + LANES), bf16),
            pltpu.VMEM((parts, seq_len, pc + LANES), bf16),
            pltpu.VMEM((parts, seq_len, 2 * pc), bf16),
            pltpu.VMEM((parts, n, rows, pc), bf16),
            pltpu.VMEM((parts, n, rows, pc), bf16),
            pltpu.VMEM((n * ndp, 1, LANES), f32),
            pltpu.VMEM((1, width), f32),
            pltpu.SMEM((heads_all,), f32),
            pltpu.VMEM((bits, width), bf16),
            pltpu.VMEM((1, bits), f32),
            dma((8,)),
            dma((2,)),
            dma((parts, nz)),
            dma((parts,)),
            dma((parts,)),
            dma((2,)),
            dma((nz,)),
            dma((2,)),
            dma((nz, nx)),
            dma((ny,)),
            dma((max(1, nz - 2), nx, ny)),
            dma((nc,)),
            dma((nc,)),
            dma((ny,)),
            dma((quarters, ny)),
            dma((nc,)),
            dma((nc,)),
            dma((quarters, max(1, ny - 1), nc)),
            dma(()),
            dma(()),
            dma((parts,)),
            dma((parts,)),
            dma(()),
            dma(()),
        ],
        compiler_params=pltpu.CompilerParams(
            collective_id=0, has_side_effects=True, vmem_limit_bytes=56 * 1024 * 1024
        ),
        name="layer",
    )(
        residual_tiles[0],
        picture_label_tile,
        prenorm_multiplier[None],
        triple_projector,
        logit_scaling,
        final_projector,
        binarizer_projector.T,
        binarizer_offset[None],
    )
    mixed, codes, ent = pl.pallas_call(
        put_kernel,
        out_shape=(
            jax.ShapeDtypeStruct((rows, width), bf16),
            jax.ShapeDtypeStruct((bits, 1, rows), f32),
            jax.ShapeDtypeStruct((1, bits), f32),
        ),
        in_specs=[vmem] * 3,
        out_specs=[hbm] * 3,
        scratch_shapes=[dma((3,))],
        name="put",
    )(*(pltpu.with_memory_space_constraint(v, pltpu.VMEM) for v in (mixed, codes, ent)))
    return mixed[None], jnp.swapaxes(codes, 0, 1), ent[0]


def solution(mesh):
    ndp, n = mesh.shape["dp"], mesh.shape["seq"]
    nx = math.isqrt(ndp // 2)
    if nx < 1 or ndp % nx:
        nx = 1
    nc = 2 if n % 2 == 0 else 1
    cfg = {"nz": ndp // nx, "nx": nx, "ny": n // nc, "nc": nc}
    return jax.shard_map(
        functools.partial(on_device, cfg),
        mesh=mesh,
        in_specs=(
            P("dp", "seq", None),
            P("dp", "seq"),
            P(),
            P("dp", None),
            P(),
            P("dp", None),
            P(),
            P(),
        ),
        out_specs=(P("dp", "seq", None), P("dp", None, "seq"), P()),
        check_vma=False,
    )
```

time: 69.4 us -> 50.9 us (0.73)
  Pallas kernels: 66.7 us -> 50.1 us
  local copies, waits for them, and re-layouts: 1.91 us -> 0 us
    pallas_call x1, Pallas kernels: 66.7 us -> 49.3 us  [on_device(): pl.pallas_call(functools.partial(layer_kernel, cfg), out_shape=(pltpu.VME...]
    unnamed x3 -> x0, local copies, waits for them, and re-layouts: 1.91 us -> none
    pallas_call x0 -> x1, Pallas kernels: none -> 0.83 us  [on_device(): pl.pallas_call(put_kernel, out_shape=(jax.ShapeDtypeStruct((rows, width),...]
where the time goes in v2:
time: 50.9 us; the launch traced here: 50.7 us
  Pallas kernels  50.1 us (98%)
  between operations  0.64 us (1%)
    pallas_call x1, Pallas kernels, on_device(): pl.pallas_call(functools.partial(layer_kernel, cfg), out_shape=(pltpu.VME...  49.3 us

profile of v2, /device:TPU:0, one launch (start us, length us, event | category | flops | bytes accessed | tf_op | source)
XLA Modules:
  0.0 50.7 jit_solution(13628790400562826725)
XLA Ops:
  0.6 49.3 %layer.1 = (bf16[256,1024]{1,0:T(8,128)(2,1)S(1)}, f32[18,1,256]{2,1,0:T(1,128)S(1)}, f32[1,18]{1,0:T(1,128)S(1)}) custom-call(bf16[256,1024]{1,0:T(8,128)(2,1)} %bitcast.7, s32[1,256]{1,0:T(1,128)} %ids_ref.1, f32[1,1024]{1,0:T(1,128)} %bitcast.9, bf16[128,3072]{1,0:T(8,128)(2,1)} %w_ref.1, f32[16]{0:T(128)} %scale_hbm.1, bf16[128,1024]{1,0:T(8,128)(2,1)} %wo_ref.1, ...), custom_call_target="tpu_custom_call" | custom-call | tf_op jit(solution)/shard_map/layer/pallas_call | solution.py:553
  49.9 0.8 %put.1 = (bf16[256,1024]{1,0:T(8,128)(2,1)}, f32[18,1,256]{2,1,0:T(1,128)}, f32[1,18]{1,0:T(1,128)}) custom-call(bf16[256,1024]{1,0:T(8,128)(2,1)S(1)} %get-tuple-element.9.mixed_ref, f32[18,1,256]{2,1,0:T(1,128)S(1)} %get-tuple-element.10.codes_ref, f32[1,18]{1,0:T(1,128)S(1)} %get-tuple-element.11.ent_ref), custom_call_target="tpu_custom_call" | custom-call | tf_op jit(solution)/shard_map/put/pallas_call | solution.py:617

commit v3 on v2

--- a/solution.py
+++ b/solution.py
@@ -47,6 +47,8 @@
     wz_r,
     wx_s,
     wx_r,
+    wt_s,
+    wt_r,
     oz_s,
     oz_r,
     ox_s,
@@ -258,9 +260,33 @@
     own_block = wg.at[:, shard_rows(z, x), :]
     pltpu.make_async_copy(own_block, own_block, local_sem.at[0]).wait()
 
+    turning = nz > 1 and nx > 1
+    last = parts - 1
+
     def w_forward(i, h):
         line_start(w_slots[h], wz_s, wz_r.at[h], i)
-        across(w_slots[h], wx_s.at[h], lambda k: wx_r.at[h], i)
+        arriving = wt_r.at[0] if turning and h == last and i == 0 else wx_r.at[h]
+        if turning and h == last and i == 1:
+
+            @pl.when(lo > 0)
+            def _():
+                across(w_slots[h], wx_s.at[h], lambda k: arriving, i)
+
+        else:
+            across(w_slots[h], wx_s.at[h], lambda k: arriving, i)
+
+    def w_rows(h, count):
+        return wg.at[h, pl.ds(0, count * (nx - 1) * shard), :]
+
+    def w_turned():
+        arrive(w_rows(last, 1), wt_r.at[0])
+        for side, wanted, zz in ((0, z == 1, z - 1), (1, z == nz - 2, z + 1)):
+
+            @pl.when(wanted)
+            def _(side=side, zz=zz):
+                for k in range(1, nx):
+                    here = w_slots[last](z, (x - k + nx) % nx)
+                    remote(here, here, wt_s.at[side], wt_r.at[1], dp_at(zz, x), me).start()
 
     for h in range(parts):
         w_forward(0, h)
@@ -339,9 +365,13 @@
         for q in range(quarters):
             events.append((((i - 1) * quarters + q + 1) * x_rows * width, 1, i, q))
     waiting = []
+    if turning:
+        events.append((parts * shard * 3 * pc + 1, 2, 0, 0))
     for _, stream, i, j in sorted(events):
         if stream == 0:
             w_arrived(i, j)
+        elif stream == 2:
+            w_turned()
         else:
             x_arrived(i, j)
             waiting.append((i, j))
@@ -368,8 +398,20 @@
         for g in range(part_heads):
             value = scale_ref[me * heads + h * part_heads + g] / math.sqrt(channel)
             scale_row = jnp.where(group_of((1, 2 * pc), 1) == g, value, scale_row)
-        if nx > 1:
-            arrive(wg.at[h, pl.ds(0, nz * (nx - 1) * shard), :], wx_r.at[h])
+        if turning and h == last:
+
+            @pl.when(lo == 0)
+            def _():
+                arrive(w_rows(h, 1), wt_r.at[1])
+                if nz > 2:
+                    arrive(w_rows(h, nz - 2), wx_r.at[h])
+
+            @pl.when(lo > 0)
+            def _():
+                arrive(w_rows(h, nz - 1), wx_r.at[h])
+
+        elif nx > 1:
+            arrive(w_rows(h, nz), wx_r.at[h])
 
         for b in range(blocks):
             r = pl.ds(b * row_block, row_block)
@@ -419,25 +461,23 @@
             if t < n - 1:
                 a2a(h, t).start()
 
-    for i in range(1, nz - 1):
-        o_line(i)
+    chores = [functools.partial(o_line, i) for i in range(1, nz - 1)]
+    for c in chores:
+        c()
+    half = n // 2
     for h in range(parts):
         project(h)
-        if h < parts - 1:
-            attend(h, range(n))
-            if h == 0 and nz > 1:
-                o_line(nz - 1)
-        else:
+        if h == 0:
             o_crossed(0)
-            attend(h, range(n // 2))
-            if parts == 1 and nz > 1:
-                o_line(nz - 1)
-            if nz > 1:
-                o_crossed(1)
-            attend(h, range(n // 2, n))
+        attend(h, range(half))
+        if h == 0 and nz > 1:
+            o_crossed(1)
+        attend(h, range(half, n))
+        if h == 0 and nz > 1:
+            o_line(nz - 1)
     for i in range(2, nz):
+        o_crossed(i)
         o_last(i - 2)
-        o_crossed(i)
     for i in range(max(0, nz - 2), nz):
         o_last(i)
     o_shared()
@@ -469,11 +509,19 @@
     stats[mine, :, :] = jnp.sum(jnp.where(lanes_eye, own_sums, 0.0), axis=0, keepdims=True)
 
     def tell(i, _):
-        t = (mine + i) % count
-        remote(stats.at[mine], stats.at[mine], st_s, st_r, t // n, t % n).start()
+        zz = jnp.where(2 * z < nz, nz - 1 - i, i)
+        for k in range(nx):
+            for m in range(n):
+                there = remote(
+                    stats.at[mine], stats.at[mine], st_s, st_r, dp_at(zz, (x + k) % nx), (me + m) % n
+                )
+                if k or m:
+                    there.start()
+                else:
+                    pl.when(zz != z)(there.start)
         return 0
 
-    lax.fori_loop(1, count, tell, 0)
+    lax.fori_loop(0, nz, tell, 0)
     others = stats.at[pl.ds(0, count - 1)]
     arrive(others, st_r)
     total = jnp.sum(stats[...], axis=0)
@@ -489,8 +537,20 @@
     line_left(lambda m: wog.at[0, :, pl.ds(0, m * shard), :], oz_s)
     halves = [i for i in range(nz) if not whole(i)]
     if nx > 1:
-        for h in range(parts):
-            left(wg.at[h, pl.ds(0, nz * (nx - 1) * shard), :], wx_s.at[h])
+        for h in range(parts - 1 if turning else parts):
+            left(w_rows(h, nz), wx_s.at[h])
+        if turning:
+            for wanted, ref, sem in (
+                (lo == 0, w_rows(last, nz - 1), wx_s.at[last]),
+                (lo > 0, w_rows(last, nz), wx_s.at[last]),
+                (z == 1, w_rows(last, 1), wt_s.at[0]),
+                (z == nz - 2, w_rows(last, 1), wt_s.at[1]),
+            ):
+
+                @pl.when(wanted)
+                def _(ref=ref, sem=sem):
+                    left(ref, sem)
+
         if halves:
             block = wog.at[0, 0, pl.ds(0, len(halves) * (nx - 1) * shard), :]
             left(block, ox_s.at[0])
@@ -581,6 +641,8 @@
             dma((parts,)),
             dma((parts,)),
             dma((2,)),
+            dma((2,)),
+            dma((2,)),
             dma((nz,)),
             dma((2,)),
             dma((nz, nx)),

time: 50.9 us -> 48.5 us (0.953)
  Pallas kernels: 50.1 us -> 47.7 us
    pallas_call x1, Pallas kernels: 49.3 us -> 46.9 us  [on_device(): pl.pallas_call(functools.partial(layer_kernel, cfg), out_shape=(pltpu.VME...]
where the time goes in v3:
time: 48.5 us; the launch traced here: 48.4 us
  Pallas kernels  47.7 us (98%)
  between operations  0.64 us (1%)
    pallas_call x1, Pallas kernels, on_device(): pl.pallas_call(functools.partial(layer_kernel, cfg), out_shape=(pltpu.VME...  46.9 us

profile of v3, /device:TPU:0, one launch (start us, length us, event | category | flops | bytes accessed | tf_op | source)
XLA Modules:
  0.0 48.4 jit_solution(7031994918458929654)
XLA Ops:
  0.6 46.9 %layer.1 = (bf16[256,1024]{1,0:T(8,128)(2,1)S(1)}, f32[18,1,256]{2,1,0:T(1,128)S(1)}, f32[1,18]{1,0:T(1,128)S(1)}) custom-call(bf16[256,1024]{1,0:T(8,128)(2,1)} %bitcast.7, s32[1,256]{1,0:T(1,128)} %ids_ref.1, f32[1,1024]{1,0:T(1,128)} %bitcast.9, bf16[128,3072]{1,0:T(8,128)(2,1)} %w_ref.1, f32[16]{0:T(128)} %scale_hbm.1, bf16[128,1024]{1,0:T(8,128)(2,1)} %wo_ref.1, ...), custom_call_target="tpu_custom_call" | custom-call | tf_op jit(solution)/shard_map/layer/pallas_call | solution.py:613
  47.5 0.8 %put.1 = (bf16[256,1024]{1,0:T(8,128)(2,1)}, f32[18,1,256]{2,1,0:T(1,128)}, f32[1,18]{1,0:T(1,128)}) custom-call(bf16[256,1024]{1,0:T(8,128)(2,1)S(1)} %get-tuple-element.9.mixed_ref, f32[18,1,256]{2,1,0:T(1,128)S(1)} %get-tuple-element.10.codes_ref, f32[1,18]{1,0:T(1,128)S(1)} %get-tuple-element.11.ent_ref), custom_call_target="tpu_custom_call" | custom-call | tf_op jit(solution)/shard_map/put/pallas_call | solution.py:679

commit v4 on v2

--- a/solution.py
+++ b/solution.py
@@ -258,12 +258,15 @@
     own_block = wg.at[:, shard_rows(z, x), :]
     pltpu.make_async_copy(own_block, own_block, local_sem.at[0]).wait()
 
-    def w_forward(i, h):
-        line_start(w_slots[h], wz_s, wz_r.at[h], i)
+    def w_along(i, h, when=True):
+        line_start(w_slots[h], wz_s, wz_r.at[h], i, when)
+
+    def w_across(i, h):
         across(w_slots[h], wx_s.at[h], lambda k: wx_r.at[h], i)
 
     for h in range(parts):
-        w_forward(0, h)
+        w_along(0, h, True if h == 0 else lo == 0)
+        w_across(0, h)
     own_id.wait()
     for i in range(1, n):
         remote(idg.at[me], idg.at[me], id_s, id_r, dp, (me + i) % n).start()
@@ -329,12 +332,16 @@
 
     def w_arrived(i, h):
         arrive(w_slots[h](piece(i), x), wz_r.at[h, piece(i)])
-        w_forward(i, h)
+        w_along(i, h)
+        w_across(i, h)
+        if (i, h) == (min(2, nz - 1), 0):
+            for later in range(1, parts):
+                w_along(0, later, lo > 0)
 
     events = []
     for i in range(1, nz):
         for h in range(parts):
-            events.append((((i - 1) * parts + h + 1) * shard * 3 * pc, 0, i, h))
+            events.append(((h * (nz - 1) + i) * shard * 3 * pc, 0, i, h))
     for i in range(1, ny):
         for q in range(quarters):
             events.append((((i - 1) * quarters + q + 1) * x_rows * width, 1, i, q))
@@ -362,6 +369,7 @@
     pair = (2 * pc, 2 * pc)
     same_head = jnp.where(group_of(pair, 0) == group_of(pair, 1), 1.0, 0.0).astype(jnp.bfloat16)
     part_heads = pc // channel
+    last = parts - 1
 
     def project(h):
         scale_row = jnp.ones((1, 2 * pc), jnp.float32)
@@ -419,25 +427,22 @@
             if t < n - 1:
                 a2a(h, t).start()
 
+    half = n // 2
+    for h in range(last):
+        project(h)
+        attend(h, range(n))
     for i in range(1, nz - 1):
         o_line(i)
-    for h in range(parts):
-        project(h)
-        if h < parts - 1:
-            attend(h, range(n))
-            if h == 0 and nz > 1:
-                o_line(nz - 1)
-        else:
-            o_crossed(0)
-            attend(h, range(n // 2))
-            if parts == 1 and nz > 1:
-                o_line(nz - 1)
-            if nz > 1:
-                o_crossed(1)
-            attend(h, range(n // 2, n))
+    o_crossed(0)
+    project(last)
+    attend(last, range(half))
+    if nz > 1:
+        o_crossed(1)
+        o_line(nz - 1)
+    attend(last, range(half, n))
     for i in range(2, nz):
+        o_crossed(i)
         o_last(i - 2)
-        o_crossed(i)
     for i in range(max(0, nz - 2), nz):
         o_last(i)
     o_shared()
@@ -469,11 +474,19 @@
     stats[mine, :, :] = jnp.sum(jnp.where(lanes_eye, own_sums, 0.0), axis=0, keepdims=True)
 
     def tell(i, _):
-        t = (mine + i) % count
-        remote(stats.at[mine], stats.at[mine], st_s, st_r, t // n, t % n).start()
+        zz = jnp.where(2 * z < nz, nz - 1 - i, i)
+        for k in range(nx):
+            for m in range(n):
+                there = remote(
+                    stats.at[mine], stats.at[mine], st_s, st_r, dp_at(zz, (x + k) % nx), (me + m) % n
+                )
+                if k or m:
+                    there.start()
+                else:
+                    pl.when(zz != z)(there.start)
         return 0
 
-    lax.fori_loop(1, count, tell, 0)
+    lax.fori_loop(0, nz, tell, 0)
     others = stats.at[pl.ds(0, count - 1)]
     arrive(others, st_r)
     total = jnp.sum(stats[...], axis=0)

time: 50.9 us -> 45.7 us (0.90)
  Pallas kernels: 50.1 us -> 45 us
    pallas_call x1, Pallas kernels: 49.3 us -> 44.1 us  [on_device(): pl.pallas_call(functools.partial(layer_kernel, cfg), out_shape=(pltpu.VME...]
where the time goes in v4:
time: 45.7 us; the launch traced here: 45.6 us
  Pallas kernels  45 us (98%)
  between operations  0.64 us (1%)
    pallas_call x1, Pallas kernels, on_device(): pl.pallas_call(functools.partial(layer_kernel, cfg), out_shape=(pltpu.VME...  44.1 us

profile of v4, /device:TPU:0, one launch (start us, length us, event | category | flops | bytes accessed | tf_op | source)
XLA Modules:
  0.0 45.6 jit_solution(2467156315811277001)
XLA Ops:
  0.6 44.1 %layer.1 = (bf16[256,1024]{1,0:T(8,128)(2,1)S(1)}, f32[18,1,256]{2,1,0:T(1,128)S(1)}, f32[1,18]{1,0:T(1,128)S(1)}) custom-call(bf16[256,1024]{1,0:T(8,128)(2,1)} %bitcast.7, s32[1,256]{1,0:T(1,128)} %ids_ref.1, f32[1,1024]{1,0:T(1,128)} %bitcast.9, bf16[128,3072]{1,0:T(8,128)(2,1)} %w_ref.1, f32[16]{0:T(128)} %scale_hbm.1, bf16[128,1024]{1,0:T(8,128)(2,1)} %wo_ref.1, ...), custom_call_target="tpu_custom_call" | custom-call | tf_op jit(solution)/shard_map/layer/pallas_call | solution.py:566
  44.8 0.8 %put.1 = (bf16[256,1024]{1,0:T(8,128)(2,1)}, f32[18,1,256]{2,1,0:T(1,128)}, f32[1,18]{1,0:T(1,128)}) custom-call(bf16[256,1024]{1,0:T(8,128)(2,1)S(1)} %get-tuple-element.9.mixed_ref, f32[18,1,256]{2,1,0:T(1,128)S(1)} %get-tuple-element.10.codes_ref, f32[1,18]{1,0:T(1,128)S(1)} %get-tuple-element.11.ent_ref), custom_call_target="tpu_custom_call" | custom-call | tf_op jit(solution)/shard_map/put/pallas_call | solution.py:630

commit v5 on v4

--- a/solution.py
+++ b/solution.py
@@ -161,7 +161,7 @@
 
     def share(here):
         for k in range(1, nc):
-            remote(here, here, oc_s.at[k], oc_r.at[k], dp, seq_at(y, (core + k) % nc)).start()
+            remote(here, here, oc_s.at[k - 1], oc_r.at[k - 1], dp, seq_at(y, (core + k) % nc)).start()
 
     def whole(i):
         return i >= nz - 2 or ny == 1
@@ -175,7 +175,7 @@
 
     def o_cross(i):
         slot = o_slot if whole(i) else lambda zz, xx: o_sub(y, zz, xx)
-        across(slot, ox_s.at[int(whole(i))], lambda k: ox_r.at[i, k], i)
+        across(slot, ox_s.at[int(whole(i))], lambda k: ox_r.at[i, k - 1], i)
 
     def o_line(i):
         p = piece(i)
@@ -187,23 +187,41 @@
     def o_crossed(i):
         for k in range(1, nx):
             here = o_crossing(i, k, 0)
-            arrive(here, ox_r.at[i, k])
+            arrive(here, ox_r.at[i, k - 1])
             if not whole(i):
                 for d in range(1, ny):
                     remote(
-                        here, here, oy_s.at[d], oy_r.at[i, k, d], dp, seq_at((y + d) % ny, core)
+                        here, here, oy_s.at[d - 1], oy_r.at[i, k - 1, d - 1], dp, seq_at((y + d) % ny, core)
                     ).start()
             share(here)
 
     def o_last(i):
         for k in range(1, nx):
             for d in range(1, 1 if whole(i) else ny):
-                arrive(o_crossing(i, k, d), oy_r.at[i, k, d])
+                arrive(o_crossing(i, k, d), oy_r.at[i, k - 1, d - 1])
                 share(o_crossing(i, k, d))
 
     def o_shared():
         for k in range(1, nc):
-            arrive(wog.at[(core - k + nc) % nc], oc_r.at[k])
+            arrive(wog.at[(core - k + nc) % nc], oc_r.at[k - 1])
+
+    barrier = pltpu.get_barrier_semaphore()
+
+    def greet(d, s):
+        pl.semaphore_signal(barrier, inc=1, device_id=(d, s), device_id_type=MESH)
+
+    for i in range(1, n):
+        greet(dp, (me + i) % n)
+    for k in range(1, nx):
+        greet(dp_at(z, (x + k) % nx), me)
+
+    @pl.when(z > 0)
+    def _():
+        greet(dp_at(z - 1, x), me)
+
+    @pl.when(z < nz - 1)
+    def _():
+        greet(dp_at(z + 1, x), me)
 
     own_w, own_o = [], []
     for h in range(parts):
@@ -212,7 +230,7 @@
                 pltpu.make_async_copy(
                     w_ref.at[:, pl.ds(pl.multiple_of(part * width + me * cols + h * pc, LANES), pc)],
                     wg.at[h, shard_rows(z, x), pl.ds(part * pc, pc)],
-                    local_sem.at[0],
+                    local_sem.at[8 + h],
                 )
             )
     own_x = pltpu.make_async_copy(x_ref, xg.at[me], local_sem.at[1])
@@ -234,30 +252,9 @@
     for c in own_w + [own_id, own_x] + own_small + own_o:
         c.start()
 
-    barrier = pltpu.get_barrier_semaphore()
-
-    def greet(d, s):
-        pl.semaphore_signal(barrier, inc=1, device_id=(d, s), device_id_type=MESH)
-
-    for i in range(1, n):
-        greet(dp, (me + i) % n)
-    for k in range(1, nx):
-        greet(dp_at(z, (x + k) % nx), me)
-
-    @pl.when(z > 0)
-    def _():
-        greet(dp_at(z - 1, x), me)
-
-    @pl.when(z < nz - 1)
-    def _():
-        greet(dp_at(z + 1, x), me)
-
     ends = jnp.where(z > 0, 1, 0) + jnp.where(z < nz - 1, 1, 0)
     pl.semaphore_wait(barrier, n - 1 + nx - 1 + ends)
 
-    own_block = wg.at[:, shard_rows(z, x), :]
-    pltpu.make_async_copy(own_block, own_block, local_sem.at[0]).wait()
-
     def w_along(i, h, when=True):
         line_start(w_slots[h], wz_s, wz_r.at[h], i, when)
 
@@ -265,6 +262,8 @@
         across(w_slots[h], wx_s.at[h], lambda k: wx_r.at[h], i)
 
     for h in range(parts):
+        own_block = w_slots[h](z, x)
+        pltpu.make_async_copy(own_block, own_block, local_sem.at[8 + h]).wait()
         w_along(0, h, True if h == 0 else lo == 0)
         w_across(0, h)
     own_id.wait()
@@ -274,9 +273,9 @@
     for q in range(quarters):
         for i in range(1, ny):
             mine = x_piece(me, q)
-            remote(mine, mine, xy_s.at[i], xy_r.at[q, i], dp, seq_at((y + i) % ny, core)).start()
+            remote(mine, mine, xy_s.at[i - 1], xy_r.at[q, i - 1], dp, seq_at((y + i) % ny, core)).start()
     for k in range(1, nc):
-        remote(xg.at[me], xg.at[me], xc_s.at[k], own_r.at[k], dp, seq_at(y, (core + k) % nc)).start()
+        remote(xg.at[me], xg.at[me], xc_s.at[k - 1], own_r.at[k - 1], dp, seq_at(y, (core + k) % nc)).start()
 
     for c in own_small:
         c.wait()
@@ -313,21 +312,21 @@
             vs[h, r, pc:] = jnp.ones((rows, pc), jnp.bfloat16)
     for k in range(1, nc):
         other = seq_at(y, (core - k + nc) % nc)
-        arrive(xg.at[other], own_r.at[k])
+        arrive(xg.at[other], own_r.at[k - 1])
         norm_rows(other, 0, quarters)
 
     def x_arrived(i, q):
         source = seq_at((y - i + ny) % ny, core)
         slot = x_piece(source, q)
-        arrive(slot, xy_r.at[q, i])
+        arrive(slot, xy_r.at[q, i - 1])
         for k in range(1, nc):
-            remote(slot, slot, xc_s.at[k], xc_r.at[q, i - 1, k], dp, seq_at(y, (core + k) % nc)).start()
+            remote(slot, slot, xc_s.at[k - 1], xc_r.at[q, i - 1, k - 1], dp, seq_at(y, (core + k) % nc)).start()
         norm_rows(source, q)
 
     def x_shared(i, q):
         for k in range(1, nc):
             other = seq_at((y - i + ny) % ny, (core - k + nc) % nc)
-            arrive(x_piece(other, q), xc_r.at[q, i - 1, k])
+            arrive(x_piece(other, q), xc_r.at[q, i - 1, k - 1])
             norm_rows(other, q)
 
     def w_arrived(i, h):
@@ -435,7 +434,8 @@
         o_line(i)
     o_crossed(0)
     project(last)
-    attend(last, range(half))
+    for t in range(half):
+        attend(last, (t,))
     if nz > 1:
         o_crossed(1)
         o_line(nz - 1)
@@ -445,17 +445,19 @@
         o_last(i - 2)
     for i in range(max(0, nz - 2), nz):
         o_last(i)
-    o_shared()
-
     for h in range(parts):
         arrive(ag.at[h, pl.ds(0, n - 1)], at_r.at[h])
         ag[h, me] = ao[h, me]
 
     attention = jnp.concatenate([ag[h, m] for m in range(n) for h in range(parts)], axis=1)
-    for g in range(nc * ny):
-        lanes = slice(g * sub, (g + 1) * sub)
-        prod = jnp.dot(attention, wog[g // ny, g % ny], preferred_element_type=jnp.float32)
-        mixed_ref[:, lanes] = (xg[me, :, lanes].astype(jnp.float32) + prod).astype(jnp.bfloat16)
+    for g in range(nc):
+        if g == 1:
+            o_shared()
+        half = (core + g) % nc
+        for yy in range(ny):
+            lanes = pl.ds(pl.multiple_of((half * ny + yy) * sub, LANES), sub)
+            prod = jnp.dot(attention, wog[half, yy], preferred_element_type=jnp.float32)
+            mixed_ref[:, lanes] = (xg[me, :, lanes].astype(jnp.float32) + prod).astype(jnp.bfloat16)
 
     logits = lax.dot_general(
         bits_ref[...], mixed_ref[...], (((1,), (1,)), ((), ())), preferred_element_type=jnp.float32
@@ -508,14 +510,14 @@
             block = wog.at[0, 0, pl.ds(0, len(halves) * (nx - 1) * shard), :]
             left(block, ox_s.at[0])
             for d in range(1, ny):
-                left(block, oy_s.at[d])
+                left(block, oy_s.at[d - 1])
         if len(halves) < nz:
             left(wog.at[0, :, pl.ds(0, (nz - len(halves)) * (nx - 1) * shard), :], ox_s.at[1])
     for k in range(1, nc):
-        left(wog.at[core], oc_s.at[k])
-        left(xg.at[pl.ds(0, ny)], xc_s.at[k])
+        left(wog.at[core], oc_s.at[k - 1])
+        left(xg.at[pl.ds(0, ny)], xc_s.at[k - 1])
     for i in range(1, ny):
-        left(xg.at[me], xy_s.at[i])
+        left(xg.at[me], xy_s.at[i - 1])
     left(idg.at[pl.ds(0, n - 1)], id_s)
     for h in range(parts):
         left(ag.at[h, pl.ds(0, n - 1)], at_s.at[h])
@@ -563,6 +565,7 @@
     dma = pltpu.SemaphoreType.DMA
     vmem, hbm = pl.BlockSpec(memory_space=pltpu.VMEM), pl.BlockSpec(memory_space=pl.ANY)
     bf16, f32 = jnp.bfloat16, jnp.float32
+    ox, oy, oc = max(1, nx - 1), max(1, ny - 1), max(1, nc - 1)
     mixed, codes, ent = pl.pallas_call(
         functools.partial(layer_kernel, cfg),
         out_shape=(
@@ -588,7 +591,7 @@
             pltpu.SMEM((heads_all,), f32),
             pltpu.VMEM((bits, width), bf16),
             pltpu.VMEM((1, bits), f32),
-            dma((8,)),
+            dma((8 + parts,)),
             dma((2,)),
             dma((parts, nz)),
             dma((parts,)),
@@ -596,16 +599,16 @@
             dma((2,)),
             dma((nz,)),
             dma((2,)),
-            dma((nz, nx)),
-            dma((ny,)),
-            dma((max(1, nz - 2), nx, ny)),
-            dma((nc,)),
-            dma((nc,)),
-            dma((ny,)),
-            dma((quarters, ny)),
-            dma((nc,)),
-            dma((nc,)),
-            dma((quarters, max(1, ny - 1), nc)),
+            dma((nz, ox)),
+            dma((oy,)),
+            dma((max(1, nz - 2), ox, oy)),
+            dma((oc,)),
+            dma((oc,)),
+            dma((oy,)),
+            dma((quarters, oy)),
+            dma((oc,)),
+            dma((oc,)),
+            dma((quarters, oy, oc)),
             dma(()),
             dma(()),
             dma((parts,)),

time: 45.7 us -> 45.2 us (0.989)
  Pallas kernels: 45 us -> 44.4 us
    pallas_call x1, Pallas kernels: 44.1 us -> 43.6 us  [on_device(): pl.pallas_call(functools.partial(layer_kernel, cfg), out_shape=(pltpu.VME...]
where the time goes in v5:
time: 45.2 us; the launch traced here: 45 us
  Pallas kernels  44.4 us (98%)
  between operations  0.64 us (1%)
    pallas_call x1, Pallas kernels, on_device(): pl.pallas_call(functools.partial(layer_kernel, cfg), out_shape=(pltpu.VME...  43.6 us

profile of v5, /device:TPU:0, one launch (start us, length us, event | category | flops | bytes accessed | tf_op | source)
XLA Modules:
  0.0 45.0 jit_solution(2963233400717975743)
XLA Ops:
  0.6 43.6 %layer.1 = (bf16[256,1024]{1,0:T(8,128)(2,1)S(1)}, f32[18,1,256]{2,1,0:T(1,128)S(1)}, f32[1,18]{1,0:T(1,128)S(1)}) custom-call(bf16[256,1024]{1,0:T(8,128)(2,1)} %bitcast.7, s32[1,256]{1,0:T(1,128)} %ids_ref.1, f32[1,1024]{1,0:T(1,128)} %bitcast.9, bf16[128,3072]{1,0:T(8,128)(2,1)} %w_ref.1, f32[16]{0:T(128)} %scale_hbm.1, bf16[128,1024]{1,0:T(8,128)(2,1)} %wo_ref.1, ...), custom_call_target="tpu_custom_call" | custom-call | tf_op jit(solution)/shard_map/layer/pallas_call | solution.py:569
  44.2 0.8 %put.1 = (bf16[256,1024]{1,0:T(8,128)(2,1)}, f32[18,1,256]{2,1,0:T(1,128)}, f32[1,18]{1,0:T(1,128)}) custom-call(bf16[256,1024]{1,0:T(8,128)(2,1)S(1)} %get-tuple-element.9.mixed_ref, f32[18,1,256]{2,1,0:T(1,128)S(1)} %get-tuple-element.10.codes_ref, f32[1,18]{1,0:T(1,128)S(1)} %get-tuple-element.11.ent_ref), custom_call_target="tpu_custom_call" | custom-call | tf_op jit(solution)/shard_map/put/pallas_call | solution.py:633

commit v6 on v5

--- a/solution.py
+++ b/solution.py
@@ -439,7 +439,8 @@
     if nz > 1:
         o_crossed(1)
         o_line(nz - 1)
-    attend(last, range(half, n))
+    for t in range(half, n):
+        attend(last, (t,))
     for i in range(2, nz):
         o_crossed(i)
         o_last(i - 2)

time: 45.2 us -> 45.2 us (level)
  no operation moved by 1% of the time
where the time goes in v6:
time: 45.2 us; the launch traced here: 45 us
  Pallas kernels  44.4 us (98%)
  between operations  0.64 us (1%)
    pallas_call x1, Pallas kernels, on_device(): pl.pallas_call(functools.partial(layer_kernel, cfg), out_shape=(pltpu.VME...  43.6 us

profile of v6, /device:TPU:0, one launch (start us, length us, event | category | flops | bytes accessed | tf_op | source)
XLA Modules:
  0.0 45.0 jit_solution(11763079316587755411)
XLA Ops:
  0.6 43.6 %layer.1 = (bf16[256,1024]{1,0:T(8,128)(2,1)S(1)}, f32[18,1,256]{2,1,0:T(1,128)S(1)}, f32[1,18]{1,0:T(1,128)S(1)}) custom-call(bf16[256,1024]{1,0:T(8,128)(2,1)} %bitcast.7, s32[1,256]{1,0:T(1,128)} %ids_ref.1, f32[1,1024]{1,0:T(1,128)} %bitcast.9, bf16[128,3072]{1,0:T(8,128)(2,1)} %w_ref.1, f32[16]{0:T(128)} %scale_hbm.1, bf16[128,1024]{1,0:T(8,128)(2,1)} %wo_ref.1, ...), custom_call_target="tpu_custom_call" | custom-call | tf_op jit(solution)/shard_map/layer/pallas_call | solution.py:570
  44.2 0.8 %put.1 = (bf16[256,1024]{1,0:T(8,128)(2,1)}, f32[18,1,256]{2,1,0:T(1,128)}, f32[1,18]{1,0:T(1,128)}) custom-call(bf16[256,1024]{1,0:T(8,128)(2,1)S(1)} %get-tuple-element.9.mixed_ref, f32[18,1,256]{2,1,0:T(1,128)S(1)} %get-tuple-element.10.codes_ref, f32[1,18]{1,0:T(1,128)S(1)} %get-tuple-element.11.ent_ref), custom_call_target="tpu_custom_call" | custom-call | tf_op jit(solution)/shard_map/put/pallas_call | solution.py:634
